TPU v7x, 32 devices: a whole 2x2x4 slice. The times are simulated.
32 devices in a mesh: corpus: 4 (over z), rerank: 8 (over y, x, core).
Axes of the slice: x: 2, y: 2, z: 4, core: 2. Of those that a mesh axis runs over, the one named last changes fastest.
Arguments:
- store_rows: bfloat16 [128, 512, 3584], P('corpus', 'rerank'), may hold values from -400 to 400
- block_lengths: int32 [128], replicated, may hold values from 128 to 512
- queries: bfloat16 [32, 64, 3584], P(None, 'rerank'), may hold values from -400 to 400
- cand_owner: int32 [64, 1], replicated, may hold values from 0 to 3; in each aligned block of 16 rows (0 to 15, 16 to 31, ...) at most 5 rows name the same one
- cand_block: int32 [64], replicated, may hold values from 0 to 31
- cand_query: int32 [64], replicated, may hold values from 0 to 31
- norm_gain: bfloat16 [3584], replicated, may hold values from 0.099609375 to 1.8984375
- w_query: bfloat16 [3584, 1792], P('rerank'), may hold values from -8 to 8
- w_key: bfloat16 [3584, 256], P('rerank'), may hold values from -1 to 1
- w_value: bfloat16 [3584, 256], P('rerank'), may hold values from -0.09375 to 0.09375
- w_score: bfloat16 [1792], replicated, may hold values from -0.125 to 0.125
Outputs:
- passage_context: bfloat16 [80, 512, 1792], P('corpus', 'rerank')
- pair_scores: float32 [64], P(('corpus', 'rerank'))
Inputs may be any that keep to these rules, and one draw needn't show every extreme that they name: `cand_owner`: at most 5 of the 16 pairs of one corpus group (an aligned block of rows) name the same owner, in every draw, some group names one owner in exactly 5 of its 16 pairs.
All inputs are finite; a program needn't handle non-finite values.
Results may differ from a plain program's by a relative error of at most 0.013.
Values may be sent and summed in bfloat16 or wider, within the bound.
A program may use at most 128 MiB of HBM per device.

v0:
```python
import functools

import jax
import jax.numpy as jnp
from jax import lax
from jax.experimental import pallas as pl
from jax.experimental.pallas import tpu as pltpu
from jax.sharding import PartitionSpec as P

HDIM = 128
QHEADS = 14
KVHEADS = 2
GROUP = QHEADS // KVHEADS
CAP = 5

ROPE_BASE = 1000000.0
EPSILON = 1e-06
NEG = -1e30
VMEM = 56 << 20


def norm_kernel(ids_ref, rows_ref, gain_ref, out_ref):
    del ids_ref
    rows = rows_ref[0].astype(jnp.float32)
    scale = lax.rsqrt(jnp.mean(rows * rows, axis=-1, keepdims=True) + EPSILON)
    out_ref[0] = (rows * scale * gain_ref[...].astype(jnp.float32)).astype(out_ref.dtype)


def pick_and_norm(table, ids, gain):
    count = ids.shape[0]
    _, rows, width = table.shape
    return pl.pallas_call(
        norm_kernel,
        out_shape=jax.ShapeDtypeStruct((count, rows, width), table.dtype),
        grid_spec=pltpu.PrefetchScalarGridSpec(
            num_scalar_prefetch=1,
            grid=(count,),
            in_specs=[
                pl.BlockSpec((1, rows, width), lambda s, ids: (ids[s], 0, 0)),
                pl.BlockSpec((1, width), lambda s, ids: (0, 0)),
            ],
            out_specs=pl.BlockSpec((1, rows, width), lambda s, ids: (s, 0, 0)),
        ),
        cost_estimate=pl.CostEstimate(
            flops=4 * count * rows * width,
            transcendentals=0,
            bytes_accessed=4 * count * rows * width,
        ),
    )(ids, table, gain)


def project_kernel(tile, rotated, x_ref, w_ref, cos_ref, sin_ref, out_ref):
    total = x_ref.shape[0]
    columns = w_ref.shape[1]

    def piece(step, rope):
        rows = pl.ds(pl.multiple_of(step * tile, tile), tile)
        raw = jnp.dot(x_ref[rows, :], w_ref[...], preferred_element_type=jnp.float32)
        if not rope:
            out_ref[rows, :] = raw.astype(out_ref.dtype)
            return
        cosine = cos_ref[rows, :]
        sine = sin_ref[rows, :]
        for head in range(columns // HDIM):
            part = raw[:, head * HDIM : (head + 1) * HDIM]
            turned = part * cosine + pltpu.roll(part, HDIM // 2, 1) * sine
            out_ref[rows, head * HDIM : (head + 1) * HDIM] = turned.astype(out_ref.dtype)

    def run(rope):
        @pl.loop(0, total // tile)
        def _(step):
            piece(step, rope)

    if rotated is None:
        run(True)
    else:

        @pl.when(pl.program_id(0) < rotated)
        def _():
            run(True)

        @pl.when(pl.program_id(0) >= rotated)
        def _():
            run(False)


def project(x, rows, w, first, columns, cosine, sine, rotated=None):
    depth = x.shape[1]
    block = 2 * HDIM
    skipped = first // block
    tile = max(t for t in range(16, 481, 16) if rows % t == 0)
    return pl.pallas_call(
        functools.partial(project_kernel, tile, rotated),
        out_shape=jax.ShapeDtypeStruct((rows, columns), x.dtype),
        grid=(columns // block,),
        in_specs=[
            pl.BlockSpec((rows, depth), lambda j: (0, 0), pipeline_mode=pl.Buffered(1)),
            pl.BlockSpec((depth, block), lambda j: (0, j + skipped)),
            pl.BlockSpec((rows, HDIM), lambda j: (0, 0), pipeline_mode=pl.Buffered(1)),
            pl.BlockSpec((rows, HDIM), lambda j: (0, 0), pipeline_mode=pl.Buffered(1)),
        ],
        out_specs=pl.BlockSpec((rows, block), lambda j: (0, j)),
        compiler_params=pltpu.CompilerParams(vmem_limit_bytes=VMEM),
        cost_estimate=pl.CostEstimate(
            flops=2 * rows * depth * columns,
            transcendentals=0,
            bytes_accessed=2 * (rows * depth + depth * columns + rows * columns),
        ),
    )(x, w, cosine, sine)


def attend_kernel(
    widths, len_ref, q_ref, kv_ref, out_ref
):
    slot = pl.program_id(0)
    member = lax.axis_index("rerank")
    length = len_ref[slot]
    chunk = q_ref.shape[0]
    start = member * chunk
    live = start < length
    keys = KVHEADS * HDIM
    scale = HDIM ** (-0.5)

    def columns(head):
        return slice(head * HDIM, (head + 1) * HDIM)

    def attend(width):
        rows = GROUP * chunk
        token = start + lax.broadcasted_iota(jnp.int32, (chunk, width), 0)
        allowed = lax.broadcasted_iota(jnp.int32, (chunk, width), 1) <= token
        allowed = jnp.concatenate([allowed.astype(jnp.float32)] * GROUP, axis=0) > 0.5
        keep = start + lax.broadcasted_iota(jnp.int32, (chunk, HDIM), 0) < length
        for head in range(KVHEADS):
            query = jnp.concatenate(
                [q_ref[:, columns(head * GROUP + g)] for g in range(GROUP)], axis=0
            )
            key = kv_ref[: width // chunk, :, columns(head)].reshape(width, HDIM)
            value = kv_ref[
                : width // chunk, :, keys + head * HDIM : keys + (head + 1) * HDIM
            ].reshape(width, HDIM)
            logits = scale * lax.dot_general(
                query, key, (((1,), (1,)), ((), ())), preferred_element_type=jnp.float32
            )
            masked = jnp.where(allowed, logits, NEG)
            weights = jnp.exp(masked - jnp.max(masked, axis=-1, keepdims=True))
            inverse = 1.0 / jnp.sum(weights, axis=-1, keepdims=True)
            probs = (weights * inverse).astype(jnp.bfloat16)
            context = jnp.dot(probs, value, preferred_element_type=jnp.float32)
            for g in range(GROUP):
                part = context[g * chunk : (g + 1) * chunk]
                out_ref[0, :, columns(head * GROUP + g)] = jnp.where(keep, part, 0.0).astype(
                    out_ref.dtype
                )

    @pl.when(jnp.logical_not(live))
    def _():
        out_ref[...] = jnp.zeros_like(out_ref)

    below = 0
    for width in widths:
        end = start + chunk

        @pl.when(live & (end > below) & (end <= width))
        def _(width=width):
            attend(width)

        below = width


def attend(lengths, chunk, query, gathered):
    slots = lengths.shape[0]
    members, _, kv_width = gathered.shape
    width = query.shape[1]
    tokens = members * chunk
    widths = [w for w in (128, 256) if w < tokens and w % chunk == 0] + [tokens]
    return pl.pallas_call(
        functools.partial(attend_kernel, widths),
        out_shape=jax.ShapeDtypeStruct((slots, chunk, width), query.dtype),
        grid_spec=pltpu.PrefetchScalarGridSpec(
            num_scalar_prefetch=1,
            grid=(slots,),
            in_specs=[
                pl.BlockSpec((chunk, width), lambda s, n: (s, 0)),
                pl.BlockSpec((members, chunk, kv_width), lambda s, n: (0, s, 0)),
            ],
            out_specs=pl.BlockSpec((1, chunk, width), lambda s, n: (s, 0, 0)),
        ),
        compiler_params=pltpu.CompilerParams(vmem_limit_bytes=VMEM),
        cost_estimate=pl.CostEstimate(
            flops=4 * slots * chunk * tokens * width,
            transcendentals=slots * chunk * QHEADS * tokens,
            bytes_accessed=2 * slots * (2 * chunk * width + tokens * kv_width),
        ),
    )(lengths, query, gathered)


def from_last(values, axis):
    members = lax.axis_size(axis)
    member = lax.axis_index(axis)
    reach = 1
    while reach < members:
        chain = [(i, i - reach) for i in range(max(members - reach, reach), members)]
        passed = lax.ppermute(values, axis, chain)
        values = jnp.where(member >= members - reach, values, passed)
        reach *= 2
    return values


def last_token(query, passage, question, alive, w_score):
    slots = query.shape[0]
    heads = query.reshape(slots, KVHEADS, GROUP, HDIM)
    both = jnp.concatenate([passage, question], axis=1)
    both = both.reshape(slots, both.shape[1], 2, KVHEADS, HDIM)
    logits = jnp.einsum(
        "skgd,stkd->skgt", heads, both[:, :, 0], preferred_element_type=jnp.float32
    ) * HDIM ** (-0.5)
    masked = jnp.where(alive[:, None, None, :], logits, NEG)
    peak = jnp.max(masked, axis=-1)
    weights = jnp.exp(masked - peak[..., None])
    total = jnp.sum(weights, axis=-1)
    context = jnp.einsum(
        "skgt,stkd->skgd",
        weights.astype(jnp.bfloat16),
        both[:, :, 1],
        preferred_element_type=jnp.float32,
    )
    gains = w_score.astype(jnp.float32).reshape(KVHEADS, GROUP, HDIM)
    part = jnp.sum(context * gains[None], axis=-1)
    return tuple(v.reshape(slots, QHEADS) for v in (peak, total, part))


def on_device(
    store_rows,
    block_lengths,
    queries,
    cand_owner,
    cand_block,
    cand_query,
    norm_gain,
    w_query,
    w_key,
    w_value,
    w_score,
):
    n_corpus = lax.axis_size("corpus")
    n_rerank = lax.axis_size("rerank")
    corpus_index = lax.axis_index("corpus")
    member = lax.axis_index("rerank")
    weights = lax.all_gather(
        jnp.concatenate([w_key, w_value, w_query], axis=1), "rerank", axis=0, tiled=True
    )
    pair_columns = w_key.shape[1] + w_value.shape[1]

    pair_total = cand_block.shape[0]
    pair_group = pair_total // n_corpus
    pair_dev = pair_group // n_rerank
    own_blocks, chunk, depth = store_rows.shape
    asking = queries.shape[1]
    owners = cand_owner[:, 0]
    pair_order = jnp.arange(pair_total, dtype=jnp.int32)
    group_of = pair_order // pair_group
    earlier = (
        (owners[:, None] == owners[None, :])
        & (group_of[:, None] == group_of[None, :])
        & (pair_order[None, :] < pair_order[:, None])
    )
    owner_rank = jnp.sum(earlier.astype(jnp.int32), axis=1)
    slots = n_corpus * CAP
    slot_ids = jnp.arange(slots, dtype=jnp.int32)
    wanted = (owners == corpus_index)[None, :] & (
        (group_of * CAP + owner_rank)[None, :] == slot_ids[:, None]
    )

    def per_slot(values):
        return jnp.sum(jnp.where(wanted, values[None, :], 0), axis=1)

    block_ids = per_slot(cand_block)
    query_ids = per_slot(cand_query)
    own_lengths = lax.dynamic_slice(block_lengths, (corpus_index * own_blocks,), (own_blocks,))
    chosen = block_ids[:, None] == jnp.arange(own_blocks, dtype=jnp.int32)[None, :]
    lengths = jnp.sum(jnp.where(chosen, own_lengths[None, :], 0), axis=1)
    lengths = jnp.where(jnp.any(wanted, axis=1), lengths, 0)

    gain = norm_gain[None, :]
    passages = pick_and_norm(store_rows, block_ids, gain)
    questions = pick_and_norm(queries, query_ids, gain)
    held = slots * chunk
    tail = from_last(queries[:, asking - 1], "rerank")
    tail = jnp.take(tail, query_ids, axis=0).astype(jnp.float32)
    scale = lax.rsqrt(jnp.mean(tail * tail, axis=-1, keepdims=True) + EPSILON)
    tail = (tail * scale * gain.astype(jnp.float32)).astype(jnp.bfloat16)
    tail_rows = pl.cdiv(slots, 16) * 16
    tail = jnp.pad(tail, ((0, tail_rows - slots), (0, 0)))
    ends = jnp.pad(lengths + (n_rerank * asking - 1), (0, tail_rows - slots))
    normed = passages.reshape(held, depth)
    questions = questions.reshape(slots * asking, depth)
    here = jnp.broadcast_to(
        (member * chunk + jnp.arange(chunk, dtype=jnp.int32))[None, :], (slots, chunk)
    )
    there = lengths[:, None] + (member * asking + jnp.arange(asking, dtype=jnp.int32))[None, :]
    positions = jnp.concatenate([here.reshape(-1), there.reshape(-1), ends])
    half = HDIM // 2
    inverse = jnp.power(ROPE_BASE, -2.0 * jnp.arange(half, dtype=jnp.float32) / HDIM)
    angles = positions.astype(jnp.float32)[:, None] * inverse
    cosine = jnp.cos(angles)
    sine = jnp.sin(angles)
    cosine = jnp.concatenate([cosine, cosine], axis=1)
    sine = jnp.concatenate([-sine, sine], axis=1)

    key_columns = w_key.shape[1]
    rotated = key_columns // (2 * HDIM)
    normed, questions, tail = lax.optimization_barrier((normed, questions, tail))
    rows = held + slots * asking
    pair_out = project(normed, held, weights, 0, pair_columns, cosine, sine, rotated)
    gathered = lax.all_gather(pair_out, "rerank", axis=0)
    ask_out = project(
        questions,
        slots * asking,
        weights,
        0,
        pair_columns,
        cosine[held:rows],
        sine[held:rows],
        rotated,
    )
    wide = w_query.shape[1]
    query_out = project(normed, held, weights, pair_columns, wide, cosine, sine)
    tail_out = project(
        tail, tail_rows, weights, pair_columns, wide, cosine[rows:], sine[rows:]
    )
    seen = (member * chunk + jnp.arange(chunk, dtype=jnp.int32))[None, :] < lengths[:, None]
    alive = jnp.concatenate([seen, jnp.ones((slots, asking), jnp.bool_)], axis=1)
    peak, total, part = last_token(
        tail_out[:slots],
        pair_out.reshape(slots, chunk, pair_columns),
        ask_out.reshape(slots, asking, pair_columns),
        alive,
        w_score,
    )

    def per_pair(values, absent):
        picked = jnp.sum(jnp.where(wanted[:, :, None], values[:, None, :], 0.0), axis=0)
        return jnp.where((owners == corpus_index)[:, None], picked, absent)

    mine = jnp.concatenate(
        [per_pair(peak, NEG), per_pair(total, 0.0), per_pair(part, 0.0)], axis=1
    )
    sources = n_corpus * n_rerank
    pieces = lax.all_to_all(
        mine.reshape(sources, pair_dev * 3 * QHEADS),
        ("corpus", "rerank"),
        split_axis=0,
        concat_axis=0,
        tiled=True,
    ).reshape(sources, pair_dev, 3, QHEADS)
    peak, total, part = pieces[:, :, 0], pieces[:, :, 1], pieces[:, :, 2]
    share = jnp.exp(peak - jnp.max(peak, axis=0, keepdims=True))
    ratio = jnp.sum(share * part, axis=0) / jnp.sum(share * total, axis=0)
    scores = jnp.sum(ratio, axis=-1)
    query_out, scores = lax.optimization_barrier((query_out, scores))
    context = attend(lengths, chunk, query_out, gathered)
    return (context, scores)


def solution(mesh):
    placed = (
        P("corpus", "rerank", None),
        P(),
        P(None, "rerank", None),
        P(),
        P(),
        P(),
        P(),
        P("rerank", None),
        P("rerank", None),
        P("rerank", None),
        P(),
    )
    return jax.shard_map(
        on_device,
        mesh=mesh,
        in_specs=placed,
        out_specs=(P("corpus", "rerank", None), P(("corpus", "rerank"))),
        check_vma=False,
    )
```

profile of v0, /device:TPU:28, one launch (start us, length us, event | category | flops | bytes accessed | tf_op | source)
XLA Modules:
  0.0 213.8 jit_solution(9945714775981843428)
XLA Ops:
  7.2 2.9 %pad_maximum_fusion = bf16[448,2304]{1,0:T(8,128)(2,1)} fusion(bf16[448,1792]{1,0:T(8,128)(2,1)} %param.18, bf16[448,256]{1,0:T(8,128)(2,1)} %param.20, bf16[448,256]{1,0:T(8,128)(2,1)} %param.19), kind=kLoop, calls=%fused_computation.1 | loop fusion | flops 6193152 | bytes 4128768 | tf_op jit(solution)/shard_map/concatenate | solution.py:250
  10.2 2.0 slice.33
  12.2 0.7 collective-permute-start
  14.1 2.7 %fusion.5 = (f32[1472,64]{1,0:T(8,128)S(1)}, f32[1472,64]{1,0:T(8,128)S(1)}, f32[1472,64]{1,0:T(8,128)S(1)}) fusion(f32[64]{0:T(128)S(1)} %multiply_power_fusion, f32[1472]{0:T(1024)S(1)} %convert_element_type.30), kind=kLoop, calls=%fused_computation.26 | loop fusion | flops 188416 | bytes 1136640 | tf_op jit(solution)/shard_map/neg | solution.py:308
  16.9 1.3 collective-permute-start.1
  18.2 1.6 pad_maximum_fusion.1
  19.8 11.4 %collective-permute-done.1 = bf16[32,3584]{1,0:T(8,128)(2,1)S(1)} collective-permute-done((bf16[32,3584]{1,0:T(8,128)(2,1)S(1)}, bf16[32,3584]{1,0:T(8,128)(2,1)S(1)}, u32[]{:S(2)}, u32[]{:S(2)}) %collective-permute-start.1) | collective-permute-done | bytes 229408 | tf_op jit(solution)/shard_map/ppermute | solution.py:203
  31.3 1.3 collective-permute-start.2
  33.2 12.1 %shard_map.123 = bf16[20,8,3584]{2,1,0:T(8,128)(2,1)} custom-call(s32[20]{0:T(128)} %copy-done.6, bf16[32,8,3584]{2,1,0:T(8,128)(2,1)} %rows_ref.3, bf16[1,3584]{1,0:T(2,128)(2,1)} %broadcast_in_dim.169.gain_ref), custom_call_target="tpu_custom_call" | custom-call | flops 2293760 | bytes 2293760 | tf_op jit(solution)/shard_map/pallas_call | solution.py:32
  45.3 17.1 %shard_map.122 = bf16[20,64,3584]{2,1,0:T(8,128)(2,1)} custom-call(s32[20]{0:T(128)} %copy-done.4, bf16[32,64,3584]{2,1,0:T(8,128)(2,1)} %rows_ref.2, bf16[1,3584]{1,0:T(2,128)(2,1)} %broadcast_in_dim.169.gain_ref), custom_call_target="tpu_custom_call" | custom-call | flops 18350080 | bytes 18350080 | tf_op jit(solution)/shard_map/pallas_call | solution.py:32
  63.5 0.7 pad.9.x_ref
  64.3 40.0 %all-gather.4.cloned.1.call-done.w_ref = bf16[3584,2304]{1,0:T(8,128)(2,1)} async-done(((bf16[448,2304]{1,0:T(8,128)(2,1)}), bf16[3584,2304]{1,0:T(8,128)(2,1)}) %all-gather.4.cloned.1.call-update) | async-done | bytes 16515088 | tf_op jit(solution)/shard_map/all_gather | solution.py:249
  104.2 11.7 %shard_map.126 = bf16[1280,512]{1,0:T(8,128)(2,1)} custom-call(bf16[1280,3584]{1,0:T(8,128)(2,1)} %bitcast.54, bf16[3584,2304]{1,0:T(8,128)(2,1)} %all-gather.4.cloned.1.call-done.w_ref, f32[1472,128]{1,0:T(8,128)} %get-tuple-element.31.cos_ref, f32[1472,128]{1,0:T(8,128)} %get-tuple-element.32.sin_ref), custom_call_target="tpu_custom_call" | custom-call | flops 4697620480 | bytes 14155776 | tf_op jit(solution)/shard_map/pallas_call | solution.py:92
  116.1 0.7 fusion.13
  116.8 0.8 fusion.9
  117.6 3.2 %concatenate.38 = bf16[20,64,2,2,128]{4,3,2,1,0:T(2,128)(2,1)S(1)} reshape(bf16[1280,512]{1,0:T(8,128)(2,1)} %shard_map.126) | data formatting | bytes 2621440 | tf_op jit(solution)/shard_map/concatenate | solution.py:212
  120.7 9.4 %shard_map.125 = bf16[32,1792]{1,0:T(8,128)(2,1)} custom-call(bf16[32,3584]{1,0:T(8,128)(2,1)} %pad.9.x_ref, bf16[3584,2304]{1,0:T(8,128)(2,1)} %all-gather.4.cloned.1.call-done.w_ref, f32[32,128]{1,0:T(8,128)} %get-tuple-element.36.cos_ref, f32[32,128]{1,0:T(8,128)} %get-tuple-element.35.sin_ref), custom_call_target="tpu_custom_call" | custom-call | flops 411041792 | bytes 13189120 | tf_op jit(solution)/shard_map/pallas_call | solution.py:92
  130.1 0.9 slice.50
  131.1 3.6 %shard_map.127 = bf16[160,512]{1,0:T(8,128)(2,1)} custom-call(bf16[160,3584]{1,0:T(8,128)(2,1)} %bitcast.57, bf16[3584,2304]{1,0:T(8,128)(2,1)} %all-gather.4.cloned.1.call-done.w_ref, f32[160,128]{1,0:T(8,128)} %get-tuple-element.34.cos_ref, f32[160,128]{1,0:T(8,128)} %get-tuple-element.33.sin_ref), custom_call_target="tpu_custom_call" | custom-call | flops 587202560 | bytes 4980736 | tf_op jit(solution)/shard_map/pallas_call | solution.py:92
  134.9 0.7 copy-done
  138.2 5.7 %all-to-all-start = ((f32[32,1,84]{2,1,0:T(1,128)}), f32[32,1,84]{2,1,0:T(1,128)S(1)}, u32[]{:S(2)}, u32[]{:S(2)}) async-start(f32[32,1,84]{2,1,0:T(1,128)} %bitcast.10), calls=%async_computation | async-start | bytes 32768 | tf_op jit(solution)/shard_map/all_to_all | solution.py:349
  143.9 28.9 %shard_map.124.q_ref = bf16[1280,1792]{1,0:T(8,128)(2,1)} custom-call(bf16[1280,3584]{1,0:T(8,128)(2,1)} %bitcast.55, bf16[3584,2304]{1,0:T(8,128)(2,1)} %all-gather.4.cloned.1.call-done.w_ref, f32[1472,128]{1,0:T(8,128)} %get-tuple-element.31.cos_ref, f32[1472,128]{1,0:T(8,128)} %get-tuple-element.32.sin_ref), custom_call_target="tpu_custom_call" | custom-call | flops 16441671680 | bytes 26607616 | tf_op jit(solution)/shard_map/pallas_call | solution.py:92
  173.8 5.8 %all-gather.6.cloned.1.call-done = bf16[10240,512]{1,0:T(8,128)(2,1)} async-done(((bf16[1280,512]{1,0:T(8,128)(2,1)}), bf16[10240,512]{1,0:T(8,128)(2,1)}) %all-gather.6.cloned.1.call-update) | async-done | bytes 10485776 | tf_op jit(solution)/shard_map/all_gather | solution.py:315
  179.6 27.4 %shard_map.128 = bf16[20,64,1792]{2,1,0:T(8,128)(2,1)} custom-call(s32[20]{0:T(128)} %copy-done.2, bf16[1280,1792]{1,0:T(8,128)(2,1)} %shard_map.124.q_ref, bf16[8,1280,512]{2,1,0:T(8,128)(2,1)} %bitcast.56), custom_call_target="tpu_custom_call" | custom-call | flops 4697620480 | bytes 19660800 | tf_op jit(solution)/shard_map/pallas_call | solution.py:176
  (83 shorter events, 6.9 us)
Async XLA Ops:
  7.2 97.1 %all-gather.4.cloned.1.call-start = ((), (), s32[]{:S(2)}) async-start(), calls=%async_computation.1 | async-start | bytes 18579456 | tf_op jit(solution)/shard_map/all_gather | solution.py:249
  10.1 2.8 %copy-start.10 = (s32[128]{0:T(128)S(1)}, s32[128]{0:T(128)}, u32[]{:S(2)}) copy-start(s32[128]{0:T(128)} %param.12) | copy-start | bytes 1540
  10.1 2.9 %copy-start.5 = (s32[64,1]{0,1:T(1,128)S(1)}, s32[64,1]{0,1:T(1,128)}, u32[]{:S(2)}) copy-start(s32[64,1]{0,1:T(1,128)} %param.14) | copy-start | bytes 772
  10.1 3.1 %copy-start.8 = (s32[64]{0:T(128)S(1)}, s32[64]{0:T(128)}, u32[]{:S(2)}) copy-start(s32[64]{0:T(128)} %param.16) | copy-start | bytes 772
  10.1 3.1 %copy-start.9 = (s32[64]{0:T(128)S(1)}, s32[64]{0:T(128)}, u32[]{:S(2)}) copy-start(s32[64]{0:T(128)} %param.15) | copy-start | bytes 772
  10.2 169.4 %all-gather.6.cloned.1.call-start = ((), (), s32[]{:S(2)}) async-start(), calls=%async_computation.2 | async-start | bytes 11796480 | tf_op jit(solution)/shard_map/all_gather | solution.py:315
  12.2 4.6 %collective-permute-start = (bf16[32,3584]{1,0:T(8,128)(2,1)S(1)}, bf16[32,3584]{1,0:T(8,128)(2,1)S(1)}, u32[]{:S(2)}, u32[]{:S(2)}) collective-permute-start(bf16[32,3584]{1,0:T(8,128)(2,1)S(1)} %bitcast.59), channel_id=1, source_target_pairs={{7,6},{15,14},{23,22},{31,30}} | collective-permute-start | bytes 688136 | tf_op jit(solution)/shard_map/ppermute | solution.py:203
  13.4 6.4 %copy-start.4 = (s32[20]{0:T(128)}, s32[20]{0:T(128)S(1)}, u32[]{:S(2)}) copy-start(s32[20]{0:T(128)S(1)} %get-tuple-element.18.ids_ref) | copy-start | bytes 244
  13.4 6.4 %copy-start.6 = (s32[20]{0:T(128)}, s32[20]{0:T(128)S(1)}, u32[]{:S(2)}) copy-start(s32[20]{0:T(128)S(1)} %get-tuple-element.17.ids_ref) | copy-start | bytes 244
  13.7 102.3 %copy-start.2 = (s32[20]{0:T(128)}, s32[20]{0:T(128)S(1)}, u32[]{:S(2)}) copy-start(s32[20]{0:T(128)S(1)} %get-tuple-element.20.len_ref) | copy-start | bytes 244
  16.9 14.4 %collective-permute-start.1 = (bf16[32,3584]{1,0:T(8,128)(2,1)S(1)}, bf16[32,3584]{1,0:T(8,128)(2,1)S(1)}, u32[]{:S(2)}, u32[]{:S(2)}) collective-permute-start(bf16[32,3584]{1,0:T(8,128)(2,1)S(1)} %broadcast_select_fusion), channel_id=1, source_target_pairs={{6,4},{7,5},{14,12},{15,13},{22,20},{23,21},{30,28},{31,29}} | collective-permute-start | bytes 688136 | tf_op jit(solution)/shard_map/ppermute | solution.py:203
  18.2 14.5 %copy-start.1 = (bf16[3584]{0:T(1024)(128)(2,1)S(1)}, bf16[3584]{0:T(1024)(128)(2,1)}, u32[]{:S(2)}) copy-start(bf16[3584]{0:T(1024)(128)(2,1)} %param.17) | copy-start | bytes 21508
  31.3 31.2 %collective-permute-start.2 = (bf16[32,3584]{1,0:T(8,128)(2,1)S(1)}, bf16[32,3584]{1,0:T(8,128)(2,1)S(1)}, u32[]{:S(2)}, u32[]{:S(2)}) collective-permute-start(bf16[32,3584]{1,0:T(8,128)(2,1)S(1)} %broadcast_select_fusion.1), channel_id=1, source_target_pairs={{4,0},{5,1},{6,2},{7,3},{12,8},{13,9},{14,10},{15,11},{20,16},{21,... | collective-permute-start | bytes 688136 | tf_op jit(solution)/shard_map/ppermute | solution.py:203
  45.3 17.2 %copy-start.7 = (s32[20]{0:T(128)S(1)}, s32[20]{0:T(128)}, u32[]{:S(2)}) copy-start(s32[20]{0:T(128)} %copy-done.6) | copy-start | bytes 244
  104.2 11.7 %copy-start.3 = (bf16[1792]{0:T(1024)(128)(2,1)S(1)}, bf16[1792]{0:T(1024)(128)(2,1)}, u32[]{:S(2)}) copy-start(bf16[1792]{0:T(1024)(128)(2,1)} %param.21) | copy-start | bytes 10756
  134.7 0.9 copy-start
  138.2 34.6 %all-to-all-start = ((f32[32,1,84]{2,1,0:T(1,128)}), f32[32,1,84]{2,1,0:T(1,128)S(1)}, u32[]{:S(2)}, u32[]{:S(2)}) async-start(f32[32,1,84]{2,1,0:T(1,128)} %bitcast.10), calls=%async_computation | async-start | bytes 32768 | tf_op jit(solution)/shard_map/all_to_all | solution.py:349
Sparse Core Ops, SparseCore 0:
  10.4 93.7 all-gather.3
  116.1 63.4 all-gather.5
where the time goes:
time: 216 us; the launch traced here: 214 us
  Pallas kernels  110 us (51%)
  waiting for transfers between devices  57.3 us (27%)
  between operations  14.4 us (7%)
  other arithmetic  11.4 us (5%)
  local copies, waits for them, and re-layouts  10.6 us (5%)
  starting transfers between devices  9.01 us (4%)
    pallas_call x4, Pallas kernels, project(): pl.pallas_call(functools.partial(project_kernel, tile, rotated), out_shap...  53.6 us
    all_gather x1, waiting for transfers between devices, on_device(): lax.all_gather(jnp.concatenate([w_key, w_value, w_query], axis=1), 'reran...  40 us
    pallas_call x2, Pallas kernels, pick_and_norm(): pl.pallas_call(norm_kernel, out_shape=jax.ShapeDtypeStruct((count, rows,...  29.2 us
    pallas_call x1, Pallas kernels, attend(): pl.pallas_call(functools.partial(attend_kernel, widths), out_shape=jax.Sh...  27.4 us
    ppermute x3, waiting for transfers between devices, from_last(): passed = lax.ppermute(values, axis, chain)  11.5 us
    all_gather x1, waiting for transfers between devices, on_device(): gathered = lax.all_gather(pair_out, 'rerank', axis=0)  5.8 us
    all_to_all x1, starting transfers between devices, on_device(): lax.all_to_all(mine.reshape(sources, pair_dev * 3 * QHEADS), ('corpus', '...  5.66 us
  transfers between devices with their start and end apart: 6, of which 3 were waited for; matrix products, arithmetic and copies ran while one was open for 9% of the time, Pallas kernels for 33%

commit v1 on v0

v1 whole, which is shorter than its diff:
```python
import functools

import jax
import jax.numpy as jnp
from jax import lax
from jax.experimental import pallas as pl
from jax.experimental.pallas import tpu as pltpu
from jax.sharding import PartitionSpec as P

HDIM = 128
QHEADS = 14
KVHEADS = 2
GROUP = QHEADS // KVHEADS
CAP = 5

ROPE_BASE = 1000000.0
EPSILON = 1e-06
NEG = -1e30
VMEM = 62 << 20


MESH = pl.DeviceIdType.MESH
WIDE = 2 * HDIM


def split_rows(rows, parts):
    unit = 16
    tiles = rows // unit
    sizes = [(tiles // parts + (p < tiles % parts)) * unit for p in range(parts)]
    starts = [sum(sizes[:p]) for p in range(parts)]
    return list(zip(starts, sizes))


def gather_project_kernel(
    plan,
    ids_ref,
    store_hbm,
    ask_ref,
    tail_hbm,
    gain_ref,
    wk_hbm,
    wv_hbm,
    wq_hbm,
    pcos_ref,
    psin_ref,
    acos_ref,
    asin_ref,
    out_hbm,
    kv_hbm,
    store,
    normed,
    weight,
    tail_raw,
    result,
    load_sem,
    own_sem,
    put_sem,
    tail_sem,
    send_sem,
    recv_sem,
):
    bits, slots, pieces, key_blocks, pair_blocks, blocks = plan
    member = lax.axis_index("rerank")
    links = list(range(1, bits))
    orders = [links[p:] + links[:p] for p in range(len(links))]
    stages = len(links)
    own_rows = wq_hbm.shape[0]
    chunk = store.shape[1]
    depth = store.shape[2]
    held = slots * chunk
    tail_rows = tail_raw.shape[0]
    total = normed.shape[0]
    piece_rows = held // pieces
    ask_rows = total - held - tail_rows

    def digit(b):
        return lax.rem(member // (2**b), 2)

    def across(b):
        return member + (1 - 2 * digit(b)) * (2**b)

    def place(spread):
        return tuple(slice(None) if b in spread else digit(b) for b in reversed(range(bits)))

    barrier = pltpu.get_barrier_semaphore()
    for b in range(bits):
        pl.semaphore_signal(
            barrier, inc=1, device_id={"rerank": across(b)}, device_id_type=MESH
        )

    own_copies = []
    for j in range(blocks):
        if j < key_blocks:
            source, column = wk_hbm, j
        elif j < pair_blocks:
            source, column = wv_hbm, j - key_blocks
        else:
            source, column = wq_hbm, j - pair_blocks
        own_copies.append(
            pltpu.make_async_copy(
                source.at[:, column * WIDE : (column + 1) * WIDE],
                weight.at[(j,) + place(())],
                own_sem.at[j],
            )
        )
        own_copies[-1].start()
    quarter = store.shape[0] // 4
    loads = [
        pltpu.make_async_copy(
            store_hbm.at[pl.ds(q * quarter, quarter)],
            store.at[pl.ds(q * quarter, quarter)],
            load_sem.at[q],
        )
        for q in range(4)
    ]
    for copy in loads:
        copy.start()
    pl.semaphore_wait(barrier, bits)

    wparts = split_rows(own_rows, stages)
    kparts = split_rows(piece_rows, stages)

    def link_copy(pairs, block, s, p):
        order = orders[p]
        if pairs:
            first, size = kparts[p]
            index = (block,) + place(order[:s]) + (slice(None), pl.ds(first, size))
            ref, at = kv_hbm, block + blocks
        else:
            first, size = wparts[p]
            index = (block,) + place(order[:s]) + (pl.ds(first, size),)
            ref, at = weight, block
        return pltpu.make_async_remote_copy(
            src_ref=ref.at[index],
            dst_ref=ref.at[index],
            send_sem=send_sem.at[at, s, p],
            recv_sem=recv_sem.at[at, s, p],
            device_id={"rerank": across(order[s])},
            device_id_type=MESH,
        )

    def core_copy(pairs, block):
        ref, at = (kv_hbm, block + blocks) if pairs else (weight, block)
        index = (block,) + place(links)
        return pltpu.make_async_remote_copy(
            src_ref=ref.at[index],
            dst_ref=ref.at[index],
            send_sem=send_sem.at[at, stages, 0],
            recv_sem=recv_sem.at[at, stages, 0],
            device_id={"rerank": across(0)},
            device_id_type=MESH,
        )

    def own_pairs(piece):
        return pltpu.make_async_copy(
            result.at[pl.ds(0, pair_blocks), pl.ds(pl.multiple_of(piece * piece_rows, 16), piece_rows)],
            kv_hbm.at[(piece,) + place(())],
            put_sem.at[piece + blocks],
        )

    def out_copy(block):
        return pltpu.make_async_copy(result.at[block], out_hbm.at[block], put_sem.at[block])

    def event(pairs, e, block):
        if e == 0 and pairs:
            own_pairs(block).wait()
        if 0 < e <= stages:
            for p in range(stages):
                link_copy(pairs, block, e - 1, p).wait_recv()
        if e < stages:
            for p in range(stages):
                link_copy(pairs, block, e, p).start()
        if e == stages:
            core_copy(pairs, block).start()
        if e == stages + 1:
            core_copy(pairs, block).wait_recv()

    def tail_copy(b):
        return pltpu.make_async_remote_copy(
            src_ref=tail_raw,
            dst_ref=tail_raw,
            send_sem=tail_sem.at[1 + b],
            recv_sem=tail_sem.at[0],
            device_id={"rerank": across(b)},
            device_id_type=MESH,
        )

    gain = gain_ref[...].astype(jnp.float32)

    def scaled(rows):
        rows = rows.astype(jnp.float32)
        scale = lax.rsqrt(jnp.mean(rows * rows, axis=-1, keepdims=True) + EPSILON)
        return (rows * scale * gain).astype(normed.dtype)

    strip = 16

    def norm_slots(lo, hi):
        @pl.loop(lo, hi)
        def _(s):
            block = ids_ref[s]
            for r in range(chunk // strip):
                row = pl.multiple_of(s * chunk + r * strip, strip)
                normed[pl.ds(row, strip), :] = scaled(store[block, r * strip : (r + 1) * strip, :])

    for copy in own_copies:
        copy.wait()
    lead = stages + 1
    cuts = [slots * i // lead for i in range(lead + 1)]
    last = 2**bits - 1

    @pl.when(member == last)
    def _():
        copy = pltpu.make_async_copy(tail_hbm, tail_raw, tail_sem.at[1 + bits])
        copy.start()
        copy.wait()

    for i in range(-lead, 0):
        for e in range(lead):
            block = i + lead - e
            if block >= 0:
                event(False, e, block)
        if i == -lead:
            for b in range(bits):
                top = 2 ** (bits - b) - 1
                if b > 0:

                    @pl.when(member // (2 ** (b - 1)) == 2 * top)
                    def _():
                        tail_copy(b - 1).wait_recv()

                @pl.when(member // (2**b) == top)
                def _():
                    tail_copy(b).start()

            @pl.loop(0, ask_rows // strip)
            def _(r):
                row = pl.multiple_of(r * strip, strip)
                normed[pl.ds(held + tail_rows + row, strip), :] = scaled(ask_ref[pl.ds(row, strip), :])

            for copy in loads:
                copy.wait()
        norm_slots(cuts[i + lead], cuts[i + lead + 1])

    @pl.when(member // (2 ** (bits - 1)) == 0)
    def _():
        tail_copy(bits - 1).wait_recv()

    for r in range(tail_rows // strip):
        normed[held + r * strip : held + (r + 1) * strip, :] = scaled(
            tail_raw[r * strip : (r + 1) * strip, :]
        )

    repeat = piece_rows // chunk

    def piece(block, start, rows, tail):
        x = normed[pl.ds(start, rows), :]
        w = weight[block].reshape(own_rows * 2**bits, WIDE)
        raw = jnp.dot(x, w, preferred_element_type=jnp.float32)
        plain = (block >= key_blocks) & (block < pair_blocks)

        def turn(part, cosine, sine):
            cosine = jnp.where(plain, 1.0, cosine)
            sine = jnp.where(plain, 0.0, sine)
            return part * cosine + pltpu.roll(part, HDIM // 2, 1) * sine

        for head in range(WIDE // HDIM):
            columns = slice(head * HDIM, (head + 1) * HDIM)
            for r in range(repeat):
                part = raw[r * chunk : (r + 1) * chunk, columns]
                result[block, pl.ds(start + r * chunk, chunk), columns] = turn(
                    part, pcos_ref[...], psin_ref[...]
                ).astype(result.dtype)
            if tail:
                result[block, held : held + tail, columns] = turn(
                    raw[piece_rows:, columns], acos_ref[:tail, :], asin_ref[:tail, :]
                ).astype(result.dtype)

    @pl.loop(0, blocks + pieces)
    def _(i):
        for e in range(lead + 1):
            block = i + lead - e

            @pl.when(block < blocks)
            def _():
                event(False, e, block)

            @pl.when((block >= blocks) & (block < blocks + pieces))
            def _():
                event(True, e, block - blocks)

        @pl.when(i < blocks)
        def _():
            @pl.loop(0, pieces - 1)
            def _(t):
                piece(i, pl.multiple_of(t * piece_rows, 16), piece_rows, 0)

        @pl.when(i < pair_blocks)
        def _():
            piece(i, held - piece_rows, piece_rows + tail_rows + ask_rows, tail_rows + ask_rows)

        @pl.when((i >= pair_blocks) & (i < blocks))
        def _():
            piece(i, held - piece_rows, piece_rows + tail_rows, tail_rows)

        @pl.when(i < blocks)
        def _():
            out_copy(i).start()

        @pl.when(i == pair_blocks - 1)
        def _():
            for p in range(pieces):
                own_pairs(p).start()

    @pl.loop(0, blocks)
    def _(j):
        out_copy(j).wait()
        for s in range(stages):
            for p in range(stages):
                link_copy(False, j, s, p).wait_send()
        core_copy(False, j).wait_send()

    @pl.loop(0, pieces)
    def _(j):
        for s in range(stages):
            for p in range(stages):
                link_copy(True, j, s, p).wait_send()
        core_copy(True, j).wait_send()

    for b in range(bits):

        @pl.when(member // (2**b) == 2 ** (bits - b) - 1)
        def _():
            tail_copy(b).wait_send()


def gather_project(ids, store, ask, tail, gain, wk, wv, wq, tables, bits, pieces):
    slots = ids.shape[0]
    _, chunk, depth = store.shape
    own_rows = wq.shape[0]
    key_blocks = wk.shape[1] // WIDE
    pair_blocks = key_blocks + wv.shape[1] // WIDE
    blocks = pair_blocks + wq.shape[1] // WIDE
    held = slots * chunk
    total = held + tail.shape[0] + ask.shape[0]
    piece_rows = held // pieces
    stages = bits - 1
    cube = (2,) * bits
    plan = (bits, slots, pieces, key_blocks, pair_blocks, blocks)
    whole = pl.BlockSpec(memory_space=pltpu.VMEM)
    apart = pl.BlockSpec(memory_space=pl.ANY)
    return pl.pallas_call(
        functools.partial(gather_project_kernel, plan),
        out_shape=(
            jax.ShapeDtypeStruct((blocks, total, WIDE), store.dtype),
            jax.ShapeDtypeStruct((pieces,) + cube + (pair_blocks, piece_rows, WIDE), store.dtype),
        ),
        in_specs=[
            pl.BlockSpec(memory_space=pltpu.SMEM),
            apart,
            whole,
            apart,
            whole,
            apart,
            apart,
            apart,
            whole,
            whole,
            whole,
            whole,
        ],
        out_specs=(apart, apart),
        scratch_shapes=[
            pltpu.VMEM(store.shape, store.dtype),
            pltpu.VMEM((total, depth), store.dtype),
            pltpu.VMEM((blocks,) + cube + (own_rows, WIDE), store.dtype),
            pltpu.VMEM(tail.shape, store.dtype),
            pltpu.VMEM((blocks, total, WIDE), store.dtype),
            pltpu.SemaphoreType.DMA((4,)),
            pltpu.SemaphoreType.DMA((blocks,)),
            pltpu.SemaphoreType.DMA((blocks + pieces,)),
            pltpu.SemaphoreType.DMA((bits + 2,)),
            pltpu.SemaphoreType.DMA((blocks + pieces, stages + 1, stages)),
            pltpu.SemaphoreType.DMA((blocks + pieces, stages + 1, stages)),
        ],
        compiler_params=pltpu.CompilerParams(
            vmem_limit_bytes=VMEM, collective_id=0, has_side_effects=True
        ),
        cost_estimate=pl.CostEstimate(
            flops=2 * total * depth * blocks * WIDE,
            transcendentals=0,
            bytes_accessed=2 * (total * depth + depth * blocks * WIDE),
        ),
    )(ids, store, ask, tail, gain, wk, wv, wq, *tables)


def attend_kernel(widths, len_ref, q_ref, kv_ref, out_ref):
    slot = pl.program_id(0)
    member = lax.axis_index("rerank")
    length = len_ref[slot]
    chunk = q_ref.shape[1]
    start = member * chunk
    live = start < length
    pair_blocks = kv_ref.shape[2]
    key_blocks = pair_blocks // 2
    scale = HDIM ** (-0.5)

    def spot(head):
        column = head * HDIM
        return column // WIDE, slice(column % WIDE, column % WIDE + HDIM)

    def attend(width):
        rows = GROUP * chunk
        token = start + lax.broadcasted_iota(jnp.int32, (chunk, width), 0)
        allowed = lax.broadcasted_iota(jnp.int32, (chunk, width), 1) <= token
        allowed = jnp.concatenate([allowed.astype(jnp.float32)] * GROUP, axis=0) > 0.5
        keep = start + lax.broadcasted_iota(jnp.int32, (chunk, HDIM), 0) < length
        for head in range(KVHEADS):
            parts = []
            for g in range(GROUP):
                block, columns = spot(head * GROUP + g)
                parts.append(q_ref[pair_blocks + block, :, columns])
            query = jnp.concatenate(parts, axis=0)
            block, columns = spot(head)
            key = kv_ref[0, : width // chunk, block, :, columns].reshape(width, HDIM)
            value = kv_ref[0, : width // chunk, key_blocks + block, :, columns].reshape(width, HDIM)
            logits = scale * lax.dot_general(
                query, key, (((1,), (1,)), ((), ())), preferred_element_type=jnp.float32
            )
            masked = jnp.where(allowed, logits, NEG)
            weights = jnp.exp(masked - jnp.max(masked, axis=-1, keepdims=True))
            inverse = 1.0 / jnp.sum(weights, axis=-1, keepdims=True)
            probs = (weights * inverse).astype(jnp.bfloat16)
            context = jnp.dot(probs, value, preferred_element_type=jnp.float32)
            for g in range(GROUP):
                part = context[g * chunk : (g + 1) * chunk]
                column = (head * GROUP + g) * HDIM
                out_ref[0, :, column : column + HDIM] = jnp.where(keep, part, 0.0).astype(
                    out_ref.dtype
                )

    @pl.when(jnp.logical_not(live))
    def _():
        out_ref[...] = jnp.zeros_like(out_ref)

    below = 0
    for width in widths:
        end = start + chunk

        @pl.when(live & (end > below) & (end <= width))
        def _(width=width):
            attend(width)

        below = width


def attend(lengths, chunk, projected, gathered):
    slots = lengths.shape[0]
    pieces, members, pair_blocks, piece_rows, _ = gathered.shape
    blocks = projected.shape[0]
    width = (blocks - pair_blocks) * WIDE
    tokens = members * chunk
    each = piece_rows // chunk
    widths = [w for w in (128, 256) if w < tokens and w % chunk == 0] + [tokens]
    return pl.pallas_call(
        functools.partial(attend_kernel, widths),
        out_shape=jax.ShapeDtypeStruct((slots, chunk, width), projected.dtype),
        grid_spec=pltpu.PrefetchScalarGridSpec(
            num_scalar_prefetch=1,
            grid=(slots,),
            in_specs=[
                pl.BlockSpec((blocks, chunk, WIDE), lambda s, n: (0, s, 0)),
                pl.BlockSpec(
                    (1, members, pair_blocks, chunk, WIDE),
                    lambda s, n: (s // each, 0, 0, s % each, 0),
                ),
            ],
            out_specs=pl.BlockSpec((1, chunk, width), lambda s, n: (s, 0, 0)),
        ),
        compiler_params=pltpu.CompilerParams(vmem_limit_bytes=48 << 20),
        cost_estimate=pl.CostEstimate(
            flops=4 * slots * chunk * tokens * width,
            transcendentals=slots * chunk * QHEADS * tokens,
            bytes_accessed=2 * slots * (2 * chunk * width + tokens * pair_blocks * WIDE),
        ),
    )(lengths, projected, gathered)


def last_token(query, passage, question, alive, w_score):
    slots = query.shape[0]
    heads = query.reshape(slots, KVHEADS, GROUP, HDIM)
    both = jnp.concatenate([passage, question], axis=1)
    both = both.reshape(slots, both.shape[1], 2, KVHEADS, HDIM)
    logits = jnp.einsum(
        "skgd,stkd->skgt", heads, both[:, :, 0], preferred_element_type=jnp.float32
    ) * HDIM ** (-0.5)
    masked = jnp.where(alive[:, None, None, :], logits, NEG)
    peak = jnp.max(masked, axis=-1)
    weights = jnp.exp(masked - peak[..., None])
    total = jnp.sum(weights, axis=-1)
    context = jnp.einsum(
        "skgt,stkd->skgd",
        weights.astype(jnp.bfloat16),
        both[:, :, 1],
        preferred_element_type=jnp.float32,
    )
    gains = w_score.astype(jnp.float32).reshape(KVHEADS, GROUP, HDIM)
    part = jnp.sum(context * gains[None], axis=-1)
    return tuple(v.reshape(slots, QHEADS) for v in (peak, total, part))


def on_device(
    store_rows,
    block_lengths,
    queries,
    cand_owner,
    cand_block,
    cand_query,
    norm_gain,
    w_query,
    w_key,
    w_value,
    w_score,
):
    n_corpus = lax.axis_size("corpus")
    n_rerank = lax.axis_size("rerank")
    corpus_index = lax.axis_index("corpus")
    member = lax.axis_index("rerank")
    pair_columns = w_key.shape[1] + w_value.shape[1]

    pair_total = cand_block.shape[0]
    pair_group = pair_total // n_corpus
    pair_dev = pair_group // n_rerank
    own_blocks, chunk, depth = store_rows.shape
    asking = queries.shape[1]
    owners = cand_owner[:, 0]
    pair_order = jnp.arange(pair_total, dtype=jnp.int32)
    group_of = pair_order // pair_group
    earlier = (
        (owners[:, None] == owners[None, :])
        & (group_of[:, None] == group_of[None, :])
        & (pair_order[None, :] < pair_order[:, None])
    )
    owner_rank = jnp.sum(earlier.astype(jnp.int32), axis=1)
    slots = n_corpus * CAP
    slot_ids = jnp.arange(slots, dtype=jnp.int32)
    wanted = (owners == corpus_index)[None, :] & (
        (group_of * CAP + owner_rank)[None, :] == slot_ids[:, None]
    )

    def per_slot(values):
        return jnp.sum(jnp.where(wanted, values[None, :], 0), axis=1)

    block_ids = per_slot(cand_block)
    query_ids = per_slot(cand_query)
    own_lengths = lax.dynamic_slice(block_lengths, (corpus_index * own_blocks,), (own_blocks,))
    chosen = block_ids[:, None] == jnp.arange(own_blocks, dtype=jnp.int32)[None, :]
    lengths = jnp.sum(jnp.where(chosen, own_lengths[None, :], 0), axis=1)
    lengths = jnp.where(jnp.any(wanted, axis=1), lengths, 0)

    gain = norm_gain[None, :]
    held = slots * chunk
    ask = jnp.take(queries, query_ids, axis=0).reshape(slots * asking, depth)
    tail = jnp.take(queries.reshape(-1, depth), query_ids * asking + asking - 1, axis=0)
    tail_rows = pl.cdiv(slots, 16) * 16
    tail = jnp.pad(tail, ((0, tail_rows - slots), (0, 0)))
    ends = jnp.pad(lengths + (n_rerank * asking - 1), (0, tail_rows - slots))
    here = member * chunk + jnp.arange(chunk, dtype=jnp.int32)
    there = lengths[:, None] + (member * asking + jnp.arange(asking, dtype=jnp.int32))[None, :]
    positions = jnp.concatenate([here, ends, there.reshape(-1)])
    half = HDIM // 2
    inverse = jnp.power(ROPE_BASE, -2.0 * jnp.arange(half, dtype=jnp.float32) / HDIM)
    angles = positions.astype(jnp.float32)[:, None] * inverse
    cosine = jnp.cos(angles)
    sine = jnp.sin(angles)
    cosine = jnp.concatenate([cosine, cosine], axis=1)
    sine = jnp.concatenate([-sine, sine], axis=1)
    tables = (cosine[:chunk], sine[:chunk], cosine[chunk:], sine[chunk:])
    bits = n_rerank.bit_length() - 1
    projected, gathered = gather_project(
        block_ids, store_rows, ask, tail, gain, w_key, w_value, w_query, tables, bits, n_corpus
    )
    pair_blocks = pair_columns // WIDE
    gathered = gathered.reshape((n_corpus, n_rerank) + gathered.shape[-3:])

    def side_by_side(values):
        return jnp.concatenate([values[i] for i in range(values.shape[0])], axis=1)

    tail_out = side_by_side(projected[pair_blocks:, held : held + slots])
    pair_out = side_by_side(projected[:pair_blocks, :held])
    ask_out = side_by_side(projected[:pair_blocks, held + tail_rows :])
    seen = (member * chunk + jnp.arange(chunk, dtype=jnp.int32))[None, :] < lengths[:, None]
    alive = jnp.concatenate([seen, jnp.ones((slots, asking), jnp.bool_)], axis=1)
    peak, total, part = last_token(
        tail_out,
        pair_out.reshape(slots, chunk, pair_columns),
        ask_out.reshape(slots, asking, pair_columns),
        alive,
        w_score,
    )

    def per_pair(values, absent):
        picked = jnp.sum(jnp.where(wanted[:, :, None], values[:, None, :], 0.0), axis=0)
        return jnp.where((owners == corpus_index)[:, None], picked, absent)

    mine = jnp.concatenate(
        [per_pair(peak, NEG), per_pair(total, 0.0), per_pair(part, 0.0)], axis=1
    )
    sources = n_corpus * n_rerank
    pieces = lax.all_to_all(
        mine.reshape(sources, pair_dev * 3 * QHEADS),
        ("corpus", "rerank"),
        split_axis=0,
        concat_axis=0,
        tiled=True,
    ).reshape(sources, pair_dev, 3, QHEADS)
    peak, total, part = pieces[:, :, 0], pieces[:, :, 1], pieces[:, :, 2]
    share = jnp.exp(peak - jnp.max(peak, axis=0, keepdims=True))
    ratio = jnp.sum(share * part, axis=0) / jnp.sum(share * total, axis=0)
    scores = jnp.sum(ratio, axis=-1)
    projected, scores = lax.optimization_barrier((projected, scores))
    context = attend(lengths, chunk, projected, gathered)
    return (context, scores)


def solution(mesh):
    placed = (
        P("corpus", "rerank", None),
        P(),
        P(None, "rerank", None),
        P(),
        P(),
        P(),
        P(),
        P("rerank", None),
        P("rerank", None),
        P("rerank", None),
        P(),
    )
    return jax.shard_map(
        on_device,
        mesh=mesh,
        in_specs=placed,
        out_specs=(P("corpus", "rerank", None), P(("corpus", "rerank"))),
        check_vma=False,
    )
```

time: 216 us -> 202 us (0.935)
  the two profiles are of different devices: /device:TPU:28 before, /device:TPU:12 now
where the time goes in v1:
time: 202 us
  Pallas kernels  161 us (80%)
  local copies, waits for them, and re-layouts  17.5 us (9%)
  blocking collectives  11 us (5%)
  other arithmetic  9.8 us (5%)
    pallas_call x1, Pallas kernels, gather_project(): pl.pallas_call(functools.partial(gather_project_kernel, plan), out_shape=...  133 us
    pallas_call x1, Pallas kernels, attend(): pl.pallas_call(functools.partial(attend_kernel, widths), out_shape=jax.Sh...  28.4 us
    all_to_all x1, blocking collectives, on_device(): lax.all_to_all(mine.reshape(sources, pair_dev * 3 * QHEADS), ('corpus', '...  11 us
    unnamed x14, local copies, waits for them, and re-layouts  4.28 us

profile of v1, /device:TPU:12, one launch (start us, length us, event | category | flops | bytes accessed | tf_op | source)
XLA Modules:
  0.0 201.7 jit_solution(13578716012303828106)
XLA Ops:
  0.7 0.8 broadcast_compare_fusion.1
  2.1 0.9 convert_reduce_fusion
  3.1 0.8 select_reduce_fusion.3
  4.0 0.7 dynamic_slice.3
  5.8 0.7 pad_maximum_fusion.2
  6.5 0.8 pad_maximum_fusion
  7.5 1.3 broadcast_in_dim.184.gain_ref
  10.9 1.2 bitcast_select_fusion.ask_ref
  12.1 133.0 %shard_map.122 = (bf16[9,1472,256]{2,1,0:T(8,128)(2,1)}, bf16[4,2,2,2,2,320,256]{6,5,4,3,2,1,0:T(8,128)(2,1)}) custom-call(s32[20]{0:T(128)} %copy-done.3, bf16[32,64,3584]{2,1,0:T(8,128)(2,1)} %store_hbm.1, bf16[160,3584]{1,0:T(8,128)(2,1)} %bitcast_select_fusion.ask_ref, bf16[32,3584]{1,0:T(8,128)(2,1)} %pad.9.tail_hbm, ...), custom_call_target="tpu_custom_call" | custom-call | flops 24310185984 | bytes 27066368 | tf_op jit(solution)/shard_map/pallas_call | solution.py:351
  145.1 0.7 constant_dynamic-update-slice_fusion.6
  145.8 0.9 slice_bitcast_fusion.1
  146.7 2.4 %fusion.19 = (bf16[1,1280,256]{2,1,0:T(8,128)(2,1)}, bf16[1,1280,256]{2,1,0:T(8,128)(2,1)}) fusion(bf16[9,1472,256]{2,1,0:T(8,128)(2,1)} %get-tuple-element.7.q_ref), kind=kLoop, calls=%fused_computation.86 | loop fusion | bytes 2621440 | tf_op jit(solution)/shard_map/slice | solution.py:586
  149.1 0.7 constant_dynamic-update-slice_fusion.5
  149.9 0.7 constant_dynamic-update-slice_fusion.4
  150.6 0.7 constant_dynamic-update-slice_fusion.3
  151.3 0.7 constant_dynamic-update-slice_fusion.2
  152.0 0.7 constant_dynamic-update-slice_fusion.1
  152.7 0.7 constant_dynamic-update-slice_fusion
  153.4 0.7 reshape.206
  154.2 1.4 maximum_maximum_fusion
  155.6 1.3 reshape.207
  156.9 2.4 %fusion.20 = (bf16[20,72,1,2,128]{4,3,2,1,0:T(2,128)(2,1)S(1)}, bf16[20,72,1,2,128]{4,3,2,1,0:T(2,128)(2,1)S(1)}) fusion(bf16[20,72,2,2,128]{4,3,2,1,0:T(2,128)(2,1)} %reshape.207), kind=kLoop, calls=%fused_computation.87 | loop fusion | bytes 2949120 | tf_op jit(solution)/shard_map/slice | solution.py:503
  161.2 11.0 %all_to_all.9 = f32[32,1,84]{2,1,0:T(1,128)S(1)} all-to-all(f32[32,1,84]{2,1,0:T(1,128)S(1)} %bitcast.78), channel_id=1, replica_groups=mesh['corpus'=4,'rerank'=8] {'corpus','rerank'}, dimensions={0} | all-to-all | bytes 21504 | tf_op jit(solution)/shard_map/all_to_all | solution.py:609
  173.2 28.4 %shard_map.123 = bf16[20,64,1792]{2,1,0:T(8,128)(2,1)} custom-call(s32[20]{0:T(128)S(1)} %get-tuple-element.18.len_ref, bf16[9,1472,256]{2,1,0:T(8,128)(2,1)} %get-tuple-element.7.q_ref, bf16[4,8,2,320,256]{4,3,2,1,0:T(8,128)(2,1)} %bitcast.75), custom_call_target="tpu_custom_call" | custom-call | flops 4697620480 | bytes 19660800 | tf_op jit(solution)/shard_map/pallas_call | solution.py:464
  (49 shorter events, 7.0 us)
Async XLA Ops:
  0.6 8.2 %copy-start = (bf16[32,8,3584]{2,1,0:T(8,128)(2,1)S(1)}, bf16[32,8,3584]{2,1,0:T(8,128)(2,1)}, u32[]{:S(2)}) copy-start(bf16[32,8,3584]{2,1,0:T(8,128)(2,1)} %param.13) | copy-start | bytes 5505028
  3.9 7.0 %copy-start.3 = (s32[20]{0:T(128)}, s32[20]{0:T(128)S(1)}, u32[]{:S(2)}) copy-start(s32[20]{0:T(128)S(1)} %get-tuple-element.16.ids_ref) | copy-start | bytes 244
  145.0 4.1 %copy-start.2 = (bf16[1792]{0:T(1024)(128)(2,1)S(1)}, bf16[1792]{0:T(1024)(128)(2,1)}, u32[]{:S(2)}) copy-start(bf16[1792]{0:T(1024)(128)(2,1)} %param.21) | copy-start | bytes 10756
  155.6 3.7 %copy-start.1 = (bf16[20,2,7,128]{3,2,1,0:T(8,128)(2,1)S(1)}, bf16[20,2,7,128]{3,2,1,0:T(8,128)(2,1)}, u32[]{:S(2)}) copy-start(bf16[20,2,7,128]{3,2,1,0:T(8,128)(2,1)} %reshape.206) | copy-start | bytes 215044

commit v2 on v1

v2 whole, which is shorter than its diff:
```python
import functools

import jax
import jax.numpy as jnp
from jax import lax
from jax.experimental import pallas as pl
from jax.experimental.pallas import tpu as pltpu
from jax.sharding import PartitionSpec as P

HDIM = 128
QHEADS = 14
KVHEADS = 2
GROUP = QHEADS // KVHEADS
CAP = 5

ROPE_BASE = 1000000.0
EPSILON = 1e-06
NEG = -1e30
VMEM = 67043328


MESH = pl.DeviceIdType.MESH
WIDE = 2 * HDIM
DIRECT = 68


def split_rows(rows, parts):
    unit = 16
    tiles = rows // unit
    sizes = [(tiles // parts + (p < tiles % parts)) * unit for p in range(parts)]
    starts = [sum(sizes[:p]) for p in range(parts)]
    return list(zip(starts, sizes))


def gather_project_kernel(
    plan,
    ids_ref,
    len_ref,
    store_hbm,
    ask_hbm,
    tail_hbm,
    gain_ref,
    wk_hbm,
    wv_hbm,
    wq_hbm,
    pcos_ref,
    psin_ref,
    acos_ref,
    asin_ref,
    gains_ref,
    out_hbm,
    stat_hbm,
    store,
    normed,
    weight,
    tail_raw,
    result,
    pairs,
    stat,
    stat_in,
    load_sem,
    own_sem,
    put_sem,
    tail_sem,
    send_sem,
    recv_sem,
    out_sem,
    stat_sem,
):
    bits, slots, pieces, key_blocks, pair_blocks, blocks, n_corpus = plan
    member = lax.axis_index("rerank")
    corpus = lax.axis_index("corpus")
    shared = n_corpus % 2 == 0
    side = lax.rem(corpus, 2) if shared else 0
    mate = corpus + 1 - 2 * side
    links = list(range(1, bits))
    orders = [links[p:] + links[:p] for p in range(len(links))]
    stages = len(links)
    own_rows = wq_hbm.shape[0]
    chunk = store.shape[1]
    depth = store.shape[2]
    held = slots * chunk
    tail_rows = tail_raw.shape[0]
    total = normed.shape[0]
    piece_rows = held // pieces
    ask_rows = total - held - tail_rows

    def digit(b):
        return lax.rem(member // (2**b), 2)

    def across(b):
        return member + (1 - 2 * digit(b)) * (2**b)

    def place(spread):
        return tuple(slice(None) if b in spread else digit(b) for b in reversed(range(bits)))

    barrier = pltpu.get_barrier_semaphore()
    for b in range(bits):
        pl.semaphore_signal(
            barrier, inc=1, device_id={"rerank": across(b)}, device_id_type=MESH
        )
    for step in range(1, n_corpus):
        pl.semaphore_signal(
            barrier,
            inc=1,
            device_id={"corpus": lax.rem(corpus + step, n_corpus)},
            device_id_type=MESH,
        )

    own_copies = []
    for j in range(blocks):
        if j < key_blocks:
            source, column = wk_hbm, j
        elif j < pair_blocks:
            source, column = wv_hbm, j - key_blocks
        else:
            source, column = wq_hbm, j - pair_blocks
        own_copies.append(
            pltpu.make_async_copy(
                source.at[:, column * WIDE : (column + 1) * WIDE],
                weight.at[(j,) + place(())],
                own_sem.at[j],
            )
        )
        own_copies[-1].start()
    quarter = store.shape[0] // 4
    loads = [
        pltpu.make_async_copy(
            store_hbm.at[pl.ds(q * quarter, quarter)],
            store.at[pl.ds(q * quarter, quarter)],
            load_sem.at[q],
        )
        for q in range(4)
    ]
    loads.append(
        pltpu.make_async_copy(
            ask_hbm, normed.at[held + tail_rows :], load_sem.at[4]
        )
    )
    for copy in loads:
        copy.start()
    pl.semaphore_wait(barrier, bits + n_corpus - 1)

    own_units = own_rows // 16
    direct = (own_units * DIRECT // 100) * 16 if shared else own_rows
    traded = own_rows - direct
    wparts = split_rows(direct, stages)
    kparts = split_rows(piece_rows, stages)

    def remote(ref, index, at, s, p, device):
        return pltpu.make_async_remote_copy(
            src_ref=ref.at[index],
            dst_ref=ref.at[index],
            send_sem=send_sem.at[at, s, p],
            recv_sem=recv_sem.at[at, s, p],
            device_id=device,
            device_id_type=MESH,
        )

    def weight_copies(block, s):
        out = []
        if s < stages:
            for p in range(stages):
                first, size = wparts[p]
                rows = pl.ds(pl.multiple_of(side * traded + first, 16), size)
                index = (block,) + place(orders[p][:s]) + (rows,)
                device = {"rerank": across(orders[p][s])}
                out.append(remote(weight, index, block, s, p, device))
        elif shared and s == stages:
            rows = pl.ds(pl.multiple_of(side * direct, 16), traded)
            for p in range(stages):
                spots = list(place(links[p + 1 :]))
                spots[bits - 1 - links[p]] = 1 - digit(links[p])
                index = (block,) + tuple(spots) + (rows,)
                out.append(remote(weight, index, block, s, p, {"corpus": mate}))
        else:
            index = (block,) + place(links)
            out.append(remote(weight, index, block, stages + 1, 0, {"rerank": across(0)}))
        return out

    def pair_copies(piece, s):
        out = []
        at = piece + blocks
        if s < stages:
            for p in range(stages):
                first, size = kparts[p]
                index = (piece,) + place(orders[p][:s]) + (slice(None), pl.ds(first, size))
                out.append(remote(pairs, index, at, s, p, {"rerank": across(orders[p][s])}))
        else:
            index = (piece,) + place(links)
            out.append(remote(pairs, index, at, stages + 1, 0, {"rerank": across(0)}))
        return out

    weight_steps = stages + 1 + shared
    pair_steps = stages + 1

    def own_pairs(piece):
        first = pl.multiple_of(piece * piece_rows, 16)
        return pltpu.make_async_copy(
            result.at[pl.ds(0, pair_blocks), pl.ds(first, piece_rows)],
            pairs.at[(piece,) + place(())],
            put_sem.at[piece],
        )

    def own_weight(block):
        return pltpu.make_async_copy(
            wq_hbm.at[:, :WIDE], weight.at[(block,) + place(())], own_sem.at[block]
        )

    def weight_event(e, block):
        if e == 0:
            own_weight(block).wait()
        else:
            for copy in weight_copies(block, e - 1):
                copy.wait_recv()
        if e < weight_steps:
            for copy in weight_copies(block, e):
                copy.start()

    def pair_event(e, piece):
        if e == 0:
            own_pairs(piece).wait()
        else:
            for copy in pair_copies(piece, e - 1):
                copy.wait_recv()
        if e < pair_steps:
            for copy in pair_copies(piece, e):
                copy.start()

    tail_order = links + [0]

    def ones(order):
        value = 1
        for b in order:
            value = value * digit(b)
        return value

    def tail_gets(t):
        return ones(tail_order[t + 1 :]) * (1 - digit(tail_order[t])) == 1

    def tail_gives(t):
        return ones(tail_order[t:]) == 1

    def tail_copy(t):
        return pltpu.make_async_remote_copy(
            src_ref=tail_raw,
            dst_ref=tail_raw,
            send_sem=tail_sem.at[1 + t],
            recv_sem=tail_sem.at[0],
            device_id={"rerank": across(tail_order[t])},
            device_id_type=MESH,
        )

    gain = gain_ref[...].astype(jnp.float32)

    def scaled(rows):
        rows = rows.astype(jnp.float32)
        scale = lax.rsqrt(jnp.mean(rows * rows, axis=-1, keepdims=True) + EPSILON)
        return (rows * scale * gain).astype(normed.dtype)

    strip = 16

    def norm_slots(lo, hi):
        @pl.loop(lo, hi)
        def _(s):
            block = ids_ref[s]
            for r in range(chunk // strip):
                row = pl.multiple_of(s * chunk + r * strip, strip)
                normed[pl.ds(row, strip), :] = scaled(store[block, r * strip : (r + 1) * strip, :])

    lead = weight_steps
    cuts = [slots * i // lead for i in range(lead + 1)]

    @pl.when(ones(tail_order) == 1)
    def _():
        copy = pltpu.make_async_copy(tail_hbm, tail_raw, tail_sem.at[1 + bits])
        copy.start()
        copy.wait()

    for i in range(-lead, 0):
        for e in range(lead):
            block = i + lead - e
            if block >= 0:
                weight_event(e, block)
        if i == -lead:
            for copy in loads:
                copy.wait()

            @pl.loop(0, ask_rows // strip)
            def _(r):
                rows = pl.ds(pl.multiple_of(held + tail_rows + r * strip, strip), strip)
                normed[rows, :] = scaled(normed[rows, :])

        norm_slots(cuts[i + lead], cuts[i + lead + 1])
        t = i + lead
        if t < bits:
            if t > 0:
                pl.when(tail_gets(t - 1))(lambda: tail_copy(t - 1).wait_recv())
            pl.when(tail_gives(t))(lambda: tail_copy(t).start())
    for t in range(min(lead, bits), bits):
        pl.when(tail_gets(t - 1))(lambda: tail_copy(t - 1).wait_recv())
        pl.when(tail_gives(t))(lambda: tail_copy(t).start())
    pl.when(tail_gets(bits - 1))(lambda: tail_copy(bits - 1).wait_recv())

    for r in range(tail_rows // strip):
        normed[held + r * strip : held + (r + 1) * strip, :] = scaled(
            tail_raw[r * strip : (r + 1) * strip, :]
        )

    repeat = piece_rows // chunk

    def piece(block, start, rows, tail):
        x = normed[pl.ds(start, rows), :]
        w = weight[block].reshape(own_rows * 2**bits, WIDE)
        raw = jnp.dot(x, w, preferred_element_type=jnp.float32)
        plain = (block >= key_blocks) & (block < pair_blocks)

        def turn(part, cosine, sine):
            cosine = jnp.where(plain, 1.0, cosine)
            sine = jnp.where(plain, 0.0, sine)
            return part * cosine + pltpu.roll(part, HDIM // 2, 1) * sine

        for head in range(WIDE // HDIM):
            columns = slice(head * HDIM, (head + 1) * HDIM)
            for r in range(repeat):
                part = raw[r * chunk : (r + 1) * chunk, columns]
                result[block, pl.ds(start + r * chunk, chunk), columns] = turn(
                    part, pcos_ref[...], psin_ref[...]
                ).astype(result.dtype)
            if tail:
                result[block, held : held + tail, columns] = turn(
                    raw[piece_rows:, columns], acos_ref[:tail, :], asin_ref[:tail, :]
                ).astype(result.dtype)

    each = piece_rows // chunk
    scale = HDIM ** (-0.5)
    lanes = stat.shape[2]
    used = GROUP * tail_rows

    def spot(head):
        column = head * HDIM
        return column // WIDE, slice(column % WIDE, column % WIDE + HDIM)

    def tail_stats():
        rows = []
        for head in range(KVHEADS):
            parts = []
            for g in range(GROUP):
                block, columns = spot(head * GROUP + g)
                parts.append(result[pair_blocks + block, held : held + tail_rows, columns])
            query = jnp.concatenate(parts, axis=0)
            block, columns = spot(head)

            def both(block):
                return jnp.concatenate(
                    [result[block, :held, columns], result[block, held + tail_rows :, columns]],
                    axis=0,
                )

            key, value = both(block), both(key_blocks + block)
            slot = lax.rem(lax.broadcasted_iota(jnp.int32, (chunk, used), 1), tail_rows)
            token = member * chunk + lax.broadcasted_iota(jnp.int32, (chunk, used), 0)
            asked = ask_rows // slots
            slot_asked = lax.rem(lax.broadcasted_iota(jnp.int32, (asked, used), 1), tail_rows)

            def logits_of(lo, hi):
                return scale * lax.dot_general(
                    key[lo:hi], query, (((1,), (1,)), ((), ())), preferred_element_type=jnp.float32
                )

            seen = jnp.full((chunk, used), NEG, jnp.float32)
            for p in range(pieces):
                logits = logits_of(p * piece_rows, (p + 1) * piece_rows)
                for u in range(each):
                    s = p * each + u
                    alive = (slot == s) & (token < len_ref[s])
                    seen = jnp.where(alive, logits[u * chunk : (u + 1) * chunk], seen)
            logits = logits_of(held, held + ask_rows)
            asks = jnp.full((asked, used), NEG, jnp.float32)
            for s in range(slots):
                asks = jnp.where(slot_asked == s, logits[s * asked : (s + 1) * asked], asks)
            peak = jnp.maximum(
                jnp.max(seen, axis=0, keepdims=True), jnp.max(asks, axis=0, keepdims=True)
            )
            seen = jnp.exp(seen - peak)
            asks = jnp.exp(asks - peak)
            total = jnp.sum(seen, axis=0, keepdims=True) + jnp.sum(asks, axis=0, keepdims=True)
            spread = [
                jnp.where(slot == s, seen, 0.0).astype(jnp.bfloat16) for s in range(slots)
            ]
            spread.append(
                jnp.concatenate(
                    [jnp.where(slot_asked == s, asks, 0.0) for s in range(slots)], axis=0
                ).astype(jnp.bfloat16)
            )
            weighed = lax.dot_general(
                gains_ref[...], value, (((1,), (1,)), ((), ())), preferred_element_type=jnp.float32
            )
            mixed = jnp.dot(
                weighed.astype(jnp.bfloat16),
                jnp.concatenate(spread, axis=0),
                preferred_element_type=jnp.float32,
            )
            which = lax.broadcasted_iota(jnp.int32, mixed.shape, 0)
            wanted = head * GROUP + lax.broadcasted_iota(jnp.int32, mixed.shape, 1) // tail_rows
            part = jnp.sum(jnp.where(which == wanted, mixed, 0.0), axis=0, keepdims=True)
            rows.append((peak, total, part))
        stat[0] = jnp.zeros((8, lanes), jnp.float32)
        for k in range(3):
            for head in range(KVHEADS):
                row = k * KVHEADS + head
                stat[0, row : row + 1, :used] = rows[head][k]

    def stat_copy(t):
        return pltpu.make_async_remote_copy(
            src_ref=stat.at[t],
            dst_ref=stat_in.at[t],
            send_sem=stat_sem.at[0, t],
            recv_sem=stat_sem.at[1, t],
            device_id={"rerank": across(t)},
            device_id_type=MESH,
        )

    def score_copy(step):
        return pltpu.make_async_remote_copy(
            src_ref=stat.at[bits],
            dst_ref=stat_hbm.at[corpus],
            send_sem=stat_sem.at[0, bits + step],
            recv_sem=stat_sem.at[1, bits + step],
            device_id={"corpus": lax.rem(corpus + step, n_corpus)},
            device_id_type=MESH,
        )

    def score_own():
        return pltpu.make_async_copy(
            stat.at[bits], stat_hbm.at[corpus], stat_sem.at[0, bits + n_corpus]
        )

    def merge_stats():
        for t in range(bits):
            stat_copy(t).start()
            stat_copy(t).wait_recv()
            mine, other = stat[t], stat_in[t]

            def rows(values, k):
                return values[k * KVHEADS : (k + 1) * KVHEADS]

            peak = jnp.maximum(rows(mine, 0), rows(other, 0))
            left = jnp.exp(rows(mine, 0) - peak)
            right = jnp.exp(rows(other, 0) - peak)
            stat[t + 1] = jnp.zeros((8, lanes), jnp.float32)
            stat[t + 1, :KVHEADS] = peak
            for k in (1, 2):
                stat[t + 1, k * KVHEADS : (k + 1) * KVHEADS] = left * rows(mine, k) + right * rows(
                    other, k
                )
        for step in range(1, n_corpus):
            score_copy(step).start()
        score_own().start()

    def attend_slot(p, u, t):
        width = chunk * 2**t
        rows = pl.ds(pl.multiple_of(p * piece_rows + u * chunk, chunk), chunk)
        inner = pl.ds(pl.multiple_of(u * chunk, chunk), chunk)
        corner = (p,) + (0,) * (bits - t) + (slice(None),) * t
        token = member * chunk + lax.broadcasted_iota(jnp.int32, (chunk, width), 0)
        allowed = lax.broadcasted_iota(jnp.int32, (chunk, width), 1) <= token
        for head in range(KVHEADS):
            spots = [spot(head * GROUP + g) for g in range(GROUP)]
            query = jnp.concatenate(
                [result[pair_blocks + block, rows, columns] for block, columns in spots], axis=0
            )
            block, columns = spot(head)
            key = pairs[corner + (block, inner, columns)].reshape(width, HDIM)
            value = pairs[corner + (key_blocks + block, inner, columns)].reshape(width, HDIM)
            logits = lax.dot_general(
                query, key, (((1,), (1,)), ((), ())), preferred_element_type=jnp.float32
            ).reshape(GROUP, chunk, width)
            masked = jnp.where(allowed[None], logits, NEG)
            peak = jnp.max(masked, axis=-1, keepdims=True)
            weights = jnp.exp(scale * (masked - peak))
            inverse = 1.0 / jnp.sum(weights, axis=-1, keepdims=True)
            context = jnp.dot(
                weights.reshape(GROUP * chunk, width).astype(jnp.bfloat16),
                value,
                preferred_element_type=jnp.float32,
            )
            context = context.reshape(GROUP, chunk, HDIM) * inverse
            for g, (block, columns) in enumerate(spots):
                result[pair_blocks + block, rows, columns] = context[g].astype(result.dtype)

    def context_copy(p, j):
        rows = pl.ds(pl.multiple_of(p * piece_rows, 16), piece_rows)
        return pltpu.make_async_copy(
            result.at[pair_blocks + j, rows],
            out_hbm.at[rows, j * WIDE : (j + 1) * WIDE],
            out_sem.at[p, j],
        )

    def attend_piece(p):
        reach = [t for t in range(bits) if chunk * 2**t >= HDIM] + [bits]
        for k, t in enumerate(reach):
            low = 0 if k == 0 else 2 ** reach[k - 1]

            @pl.when((member >= low) & (member < 2**t))
            def _():
                @pl.loop(0, each)
                def _(u):
                    attend_slot(p, u, t)

        for j in range(blocks - pair_blocks):
            context_copy(p, j).start()

    begin = max(blocks - pair_steps - 1, pair_blocks)
    finish = begin + pieces + pair_steps

    @pl.loop(0, finish)
    def _(i):
        for e in range(weight_steps + 1):
            block = i + lead - e

            @pl.when(block < blocks)
            def _():
                weight_event(e, block)

        for e in range(pair_steps + 1):
            place_of = i - begin - e

            @pl.when((place_of >= 0) & (place_of < pieces))
            def _():
                pair_event(e, place_of)

        @pl.when(i < blocks)
        def _():
            @pl.loop(0, pieces - 1)
            def _(t):
                piece(i, pl.multiple_of(t * piece_rows, 16), piece_rows, 0)

        @pl.when(i < pair_blocks)
        def _():
            piece(i, held - piece_rows, piece_rows + tail_rows + ask_rows, tail_rows + ask_rows)

        @pl.when((i >= pair_blocks) & (i < blocks))
        def _():
            piece(i, held - piece_rows, piece_rows + tail_rows, tail_rows)

        @pl.when(i == pair_blocks - 1)
        def _():
            for p in range(pieces):
                own_pairs(p).start()

        @pl.when(i == blocks - 1)
        def _():
            tail_stats()

        @pl.when(i == blocks)
        def _():
            merge_stats()

        done = i - begin - pair_steps

        @pl.when(done >= 0)
        def _():
            attend_piece(done)

    for step in range(1, n_corpus):
        score_copy(step).wait()
    score_own().wait()
    for t in range(bits):
        stat_copy(t).wait_send()

    @pl.loop(0, blocks)
    def _(j):
        for s in range(weight_steps):
            for copy in weight_copies(j, s):
                copy.wait_send()

    @pl.loop(0, pieces)
    def _(p):
        for s in range(pair_steps):
            for copy in pair_copies(p, s):
                copy.wait_send()
        for j in range(blocks - pair_blocks):
            context_copy(p, j).wait()

    for t in range(bits):
        pl.when(tail_gives(t))(lambda: tail_copy(t).wait_send())


def fused(ids, lengths, store, ask, tail, gain, wk, wv, wq, tables, gains, bits, n_corpus):
    slots = ids.shape[0]
    pieces = n_corpus
    _, chunk, depth = store.shape
    own_rows = wq.shape[0]
    key_blocks = wk.shape[1] // WIDE
    pair_blocks = key_blocks + wv.shape[1] // WIDE
    blocks = pair_blocks + wq.shape[1] // WIDE
    held = slots * chunk
    total = held + tail.shape[0] + ask.shape[0]
    piece_rows = held // pieces
    stages = bits - 1
    cube = (2,) * bits
    lanes = pl.cdiv(GROUP * tail.shape[0], 128) * 128
    plan = (bits, slots, pieces, key_blocks, pair_blocks, blocks, n_corpus)
    whole = pl.BlockSpec(memory_space=pltpu.VMEM)
    apart = pl.BlockSpec(memory_space=pl.ANY)
    scalar = pl.BlockSpec(memory_space=pltpu.SMEM)
    return pl.pallas_call(
        functools.partial(gather_project_kernel, plan),
        out_shape=(
            jax.ShapeDtypeStruct((held, wq.shape[1]), store.dtype),
            jax.ShapeDtypeStruct((n_corpus, 8, lanes), jnp.float32),
        ),
        in_specs=[scalar, scalar, apart, apart, apart, whole, apart, apart, apart]
        + [whole] * (len(tables) + 1),
        out_specs=(apart, apart),
        scratch_shapes=[
            pltpu.VMEM(store.shape, store.dtype),
            pltpu.VMEM((total, depth), store.dtype),
            pltpu.VMEM((blocks,) + cube + (own_rows, WIDE), store.dtype),
            pltpu.VMEM(tail.shape, store.dtype),
            pltpu.VMEM((blocks, total, WIDE), store.dtype),
            pltpu.VMEM((pieces,) + cube + (pair_blocks, piece_rows, WIDE), store.dtype),
            pltpu.VMEM((bits + 1, 8, lanes), jnp.float32),
            pltpu.VMEM((bits, 8, lanes), jnp.float32),
            pltpu.SemaphoreType.DMA((5,)),
            pltpu.SemaphoreType.DMA((blocks,)),
            pltpu.SemaphoreType.DMA((pieces,)),
            pltpu.SemaphoreType.DMA((bits + 2,)),
            pltpu.SemaphoreType.DMA((blocks + pieces, stages + 2, stages)),
            pltpu.SemaphoreType.DMA((blocks + pieces, stages + 2, stages)),
            pltpu.SemaphoreType.DMA((pieces, blocks - pair_blocks)),
            pltpu.SemaphoreType.DMA((2, bits + n_corpus + 1)),
        ],
        compiler_params=pltpu.CompilerParams(
            vmem_limit_bytes=VMEM, collective_id=0, has_side_effects=True
        ),
        cost_estimate=pl.CostEstimate(
            flops=2 * total * depth * blocks * WIDE,
            transcendentals=0,
            bytes_accessed=2 * (total * depth + depth * blocks * WIDE),
        ),
    )(ids, lengths, store, ask, tail, gain, wk, wv, wq, *tables, gains)


def on_device(
    store_rows,
    block_lengths,
    queries,
    cand_owner,
    cand_block,
    cand_query,
    norm_gain,
    w_query,
    w_key,
    w_value,
    w_score,
):
    n_corpus = lax.axis_size("corpus")
    n_rerank = lax.axis_size("rerank")
    corpus_index = lax.axis_index("corpus")
    member = lax.axis_index("rerank")

    pair_total = cand_block.shape[0]
    pair_group = pair_total // n_corpus
    pair_dev = pair_group // n_rerank
    own_blocks, chunk, depth = store_rows.shape
    asking = queries.shape[1]
    owners = cand_owner[:, 0]
    pair_order = jnp.arange(pair_total, dtype=jnp.int32)
    group_of = pair_order // pair_group
    earlier = (
        (owners[:, None] == owners[None, :])
        & (group_of[:, None] == group_of[None, :])
        & (pair_order[None, :] < pair_order[:, None])
    )
    owner_rank = jnp.sum(earlier.astype(jnp.int32), axis=1)
    slots = n_corpus * CAP
    slot_ids = jnp.arange(slots, dtype=jnp.int32)
    wanted = (owners == corpus_index)[None, :] & (
        (group_of * CAP + owner_rank)[None, :] == slot_ids[:, None]
    )

    def per_slot(values):
        return jnp.sum(jnp.where(wanted, values[None, :], 0), axis=1)

    block_ids = per_slot(cand_block)
    query_ids = per_slot(cand_query)
    own_lengths = lax.dynamic_slice(block_lengths, (corpus_index * own_blocks,), (own_blocks,))
    chosen = block_ids[:, None] == jnp.arange(own_blocks, dtype=jnp.int32)[None, :]
    lengths = jnp.sum(jnp.where(chosen, own_lengths[None, :], 0), axis=1)
    lengths = jnp.where(jnp.any(wanted, axis=1), lengths, 0)

    gain = norm_gain[None, :]
    held = slots * chunk
    ask = jnp.take(queries, query_ids, axis=0).reshape(slots * asking, depth)
    tail = jnp.take(queries.reshape(-1, depth), query_ids * asking + asking - 1, axis=0)
    tail_rows = pl.cdiv(slots, 16) * 16
    tail = jnp.pad(tail, ((0, tail_rows - slots), (0, 0)))
    ends = jnp.pad(lengths + (n_rerank * asking - 1), (0, tail_rows - slots))
    here = member * chunk + jnp.arange(chunk, dtype=jnp.int32)
    there = lengths[:, None] + (member * asking + jnp.arange(asking, dtype=jnp.int32))[None, :]
    positions = jnp.concatenate([here, ends, there.reshape(-1)])
    half = HDIM // 2
    inverse = jnp.power(ROPE_BASE, -2.0 * jnp.arange(half, dtype=jnp.float32) / HDIM)
    angles = positions.astype(jnp.float32)[:, None] * inverse
    cosine = jnp.cos(angles)
    sine = jnp.sin(angles)
    cosine = jnp.concatenate([cosine, cosine], axis=1)
    sine = jnp.concatenate([-sine, sine], axis=1)
    tables = (cosine[:chunk], sine[:chunk], cosine[chunk:], sine[chunk:])
    bits = n_rerank.bit_length() - 1
    gains = w_score.reshape(QHEADS, HDIM)
    context, stats = fused(
        block_ids,
        lengths,
        store_rows,
        ask,
        tail,
        gain,
        w_key,
        w_value,
        w_query,
        tables,
        gains,
        bits,
        n_corpus,
    )
    wide = context.shape[1]
    here = member * chunk + jnp.arange(chunk, dtype=jnp.int32)
    keep = here[None, :, None] < lengths[:, None, None]
    context = jnp.where(keep, context.reshape(slots, chunk, wide), 0)
    used = GROUP * tail_rows
    ratio = stats[:, 2 * KVHEADS : 3 * KVHEADS, :used] / stats[:, KVHEADS : 2 * KVHEADS, :used]
    ratio = ratio.reshape(n_corpus, KVHEADS * GROUP, tail_rows).sum(axis=1)[:, :slots]
    first = corpus_index * pair_group + member * pair_dev
    mine = first + jnp.arange(pair_dev, dtype=jnp.int32)
    is_mine = mine[:, None] == pair_order[None, :]

    def of_mine(values):
        return jnp.sum(jnp.where(is_mine, values[None, :], 0), axis=1)

    place = of_mine(owners) * slots + corpus_index * CAP + of_mine(owner_rank)
    spread = jnp.arange(n_corpus * slots, dtype=jnp.int32)
    scores = jnp.sum(
        jnp.where(place[:, None] == spread[None, :], ratio.reshape(1, -1), 0.0), axis=1
    )
    return (context, scores)


def solution(mesh):
    placed = (
        P("corpus", "rerank", None),
        P(),
        P(None, "rerank", None),
        P(),
        P(),
        P(),
        P(),
        P("rerank", None),
        P("rerank", None),
        P("rerank", None),
        P(),
    )
    return jax.shard_map(
        on_device,
        mesh=mesh,
        in_specs=placed,
        out_specs=(P("corpus", "rerank", None), P(("corpus", "rerank"))),
        check_vma=False,
    )
```

time: 202 us -> 149 us (0.74)
  the two profiles are of different devices: /device:TPU:12 before, /device:TPU:28 now
where the time goes in v2:
time: 149 us; the launch traced here: 147 us
  Pallas kernels  125 us (84%)
  other arithmetic  13.9 us (9%)
  local copies, waits for them, and re-layouts  6.75 us (5%)
    pallas_call x1, Pallas kernels, fused(): pl.pallas_call(functools.partial(gather_project_kernel, plan), out_shape=...  125 us
    select_n x1, other arithmetic, on_device(): context = jnp.where(keep, context.reshape(slots, chunk, wide), 0)  4.84 us

profile of v2, /device:TPU:28, one launch (start us, length us, event | category | flops | bytes accessed | tf_op | source)
XLA Modules:
  0.0 146.5 jit_solution(13723639182296006047)
XLA Ops:
  0.7 0.7 broadcast_compare_fusion.1
  1.3 0.7 dynamic_slice.3
  2.1 0.9 convert_reduce_fusion
  3.0 0.9 select_reduce_fusion.4
  3.9 0.6 add_add_fusion
  4.5 0.1 fusion.3
  4.6 0.8 select_reduce_fusion
  5.4 0.2 select_reduce_fusion.1
  5.6 0.3 copy-done.4
  6.0 0.1 broadcast_in_dim.138
  6.1 0.7 broadcast_compare_fusion
  6.8 0.1 add.174
  7.0 1.3 broadcast_in_dim.144.gain_ref
  8.3 2.6 %gather_fusion.1 = bf16[20,3584]{1,0:T(8,128)(2,1)S(1)} fusion(bf16[256,3584]{1,0:T(8,128)(2,1)} %bitcast.18, s32[1024]{0:T(1024)S(1)} %get-tuple-element.19), kind=kCustom, calls=%fused_computation.1 | custom fusion | bytes 286800 | tf_op jit(solution)/shard_map/jit(_take)/gather | solution.py:697
  10.9 0.1 broadcast_select_fusion.1
  11.0 0.7 pad.8.tail_hbm
  11.8 0.5 fusion
  12.3 0.7 pad_maximum_fusion.2
  13.0 0.8 pad_maximum_fusion
  13.8 0.6 gather_fusion
  14.4 1.2 bitcast_select_fusion.ask_hbm
  15.6 125.1 %shard_map.122 = (bf16[1280,1792]{1,0:T(8,128)(2,1)}, f32[4,8,256]{2,1,0:T(8,128)}) custom-call(s32[20]{0:T(128)} %copy-done.4, s32[20]{0:T(128)} %copy-done.2, bf16[32,64,3584]{2,1,0:T(8,128)(2,1)} %store_hbm.1, bf16[160,3584]{1,0:T(8,128)(2,1)} %bitcast_select_fusion.ask_hbm, bf16[32,3584]{1,0:T(8,128)(2,1)} %pad.8.tail_hbm, ...), custom_call_target="tpu_custom_call" | custom-call | flops 24310185984 | bytes 27066368 | tf_op jit(solution)/shard_map/pallas_call | solution.py:608
  140.8 4.8 %broadcast_select_fusion = bf16[20,64,1792]{2,1,0:T(8,128)(2,1)} fusion(bf16[20,64,1792]{2,1,0:T(8,128)(2,1)} %bitcast.17, pred[20,64]{1,0:T(8,128)(4,1)} %broadcast_compare_fusion), kind=kLoop, calls=%fused_computation.2 | loop fusion | flops 2293760 | bytes 9176320 | tf_op jit(solution)/shard_map/jit(_where)/select_n | solution.py:732
  145.8 0.7 fusion.4
  (26 shorter events, 0.5 us)
Async XLA Ops:
  5.4 0.5 copy-start.4
  5.6 8.2 %copy-start.2 = (s32[20]{0:T(128)}, s32[20]{0:T(128)S(1)}, u32[]{:S(2)}) copy-start(s32[20]{0:T(128)S(1)} %get-tuple-element.11.len_ref) | copy-start | bytes 244
  8.3 5.5 %copy-start = (bf16[32,8,3584]{2,1,0:T(8,128)(2,1)S(1)}, bf16[32,8,3584]{2,1,0:T(8,128)(2,1)}, u32[]{:S(2)}) copy-start(bf16[32,8,3584]{2,1,0:T(8,128)(2,1)} %param.13) | copy-start | bytes 5505028
  140.7 4.9 %copy-start.1 = (f32[4,8,256]{2,1,0:T(8,128)S(1)}, f32[4,8,256]{2,1,0:T(8,128)}, u32[]{:S(2)}) copy-start(f32[4,8,256]{2,1,0:T(8,128)} %get-tuple-element.5) | copy-start | bytes 98308
  140.7 5.1 %copy-start.3 = (s32[2]{0:T(128)S(1)}, s32[2]{0:T(128)}, u32[]{:S(2)}) copy-start(s32[2]{0:T(128)} %add_add_fusion) | copy-start | bytes 28

commit v3 on v2

--- a/solution.py
+++ b/solution.py
@@ -22,6 +22,8 @@
 MESH = pl.DeviceIdType.MESH
 WIDE = 2 * HDIM
 DIRECT = 68
+AHEAD = 2
+WAIT = 3
 
 
 def split_rows(rows, parts):
@@ -34,30 +36,36 @@
 
 def gather_project_kernel(
     plan,
-    ids_ref,
-    len_ref,
+    owner_ref,
+    pick_ref,
+    ask_ref,
+    length_ref,
     store_hbm,
-    ask_hbm,
-    tail_hbm,
+    query_hbm,
     gain_ref,
     wk_hbm,
     wv_hbm,
     wq_hbm,
+    inverse_ref,
+    gains_ref,
+    out_hbm,
+    score_ref,
+    ids_ref,
+    len_ref,
+    query_ids,
+    store,
+    queries,
+    normed,
+    weight,
+    result,
+    pairs,
     pcos_ref,
     psin_ref,
     acos_ref,
     asin_ref,
-    gains_ref,
-    out_hbm,
-    stat_hbm,
-    store,
-    normed,
-    weight,
-    tail_raw,
-    result,
-    pairs,
     stat,
     stat_in,
+    stat_all,
     load_sem,
     own_sem,
     put_sem,
@@ -67,7 +75,7 @@
     out_sem,
     stat_sem,
 ):
-    bits, slots, pieces, key_blocks, pair_blocks, blocks, n_corpus = plan
+    bits, slots, pieces, tiles, key_blocks, pair_blocks, blocks, n_corpus = plan
     member = lax.axis_index("rerank")
     corpus = lax.axis_index("corpus")
     shared = n_corpus % 2 == 0
@@ -80,8 +88,8 @@
     chunk = store.shape[1]
     depth = store.shape[2]
     held = slots * chunk
-    tail_rows = tail_raw.shape[0]
     total = normed.shape[0]
+    tail_rows = pl.cdiv(slots, 16) * 16
     piece_rows = held // pieces
     ask_rows = total - held - tail_rows
 
@@ -132,13 +140,31 @@
         )
         for q in range(4)
     ]
-    loads.append(
-        pltpu.make_async_copy(
-            ask_hbm, normed.at[held + tail_rows :], load_sem.at[4]
-        )
-    )
+    loads.append(pltpu.make_async_copy(query_hbm, queries, load_sem.at[4]))
     for copy in loads:
         copy.start()
+    pair_group = owner_ref.shape[0] // n_corpus
+
+    @pl.loop(0, n_corpus)
+    def _(g):
+        def look(q, carry):
+            count, picks, asks = carry
+            p = g * pair_group + q
+            mine = owner_ref[p] == corpus
+            picks = tuple(
+                jnp.where(mine & (count == r), pick_ref[p], v) for r, v in enumerate(picks)
+            )
+            asks = tuple(jnp.where(mine & (count == r), ask_ref[p], v) for r, v in enumerate(asks))
+            return count + jnp.where(mine, 1, 0), picks, asks
+
+        none = (jnp.int32(0),) * CAP
+        count, picks, asks = lax.fori_loop(0, pair_group, look, (jnp.int32(0), none, none))
+        for r in range(CAP):
+            ids_ref[g * CAP + r] = picks[r]
+            query_ids[g * CAP + r] = asks[r]
+            length = length_ref[corpus * store.shape[0] + picks[r]]
+            len_ref[g * CAP + r] = jnp.where(count > r, length, 0)
+
     pl.semaphore_wait(barrier, bits + n_corpus - 1)
 
     own_units = own_rows // 16
@@ -243,15 +269,15 @@
 
     def tail_copy(t):
         return pltpu.make_async_remote_copy(
-            src_ref=tail_raw,
-            dst_ref=tail_raw,
+            src_ref=normed.at[held : held + tail_rows],
+            dst_ref=normed.at[held : held + tail_rows],
             send_sem=tail_sem.at[1 + t],
             recv_sem=tail_sem.at[0],
             device_id={"rerank": across(tail_order[t])},
             device_id_type=MESH,
         )
 
-    gain = gain_ref[...].astype(jnp.float32)
+    gain = gain_ref[...].astype(jnp.float32).reshape(1, depth)
 
     def scaled(rows):
         rows = rows.astype(jnp.float32)
@@ -271,25 +297,59 @@
     lead = weight_steps
     cuts = [slots * i // lead for i in range(lead + 1)]
 
-    @pl.when(ones(tail_order) == 1)
-    def _():
-        copy = pltpu.make_async_copy(tail_hbm, tail_raw, tail_sem.at[1 + bits])
-        copy.start()
-        copy.wait()
-
+    asking = queries.shape[1]
+
+    def asked_rows(s):
+        return queries[query_ids[s]].astype(jnp.float32)
+
+    def tables():
+        def turn(positions):
+            angles = positions.astype(jnp.float32) * inverse_ref[...]
+            lane = lax.broadcasted_iota(jnp.int32, angles.shape, 1)
+            sine = jnp.sin(angles)
+            return jnp.cos(angles), jnp.where(lane < HDIM // 2, -sine, sine)
+
+        here = lax.broadcasted_iota(jnp.int32, (chunk, HDIM), 0)
+        pcos_ref[...], psin_ref[...] = turn(member * chunk + here)
+        row = lax.broadcasted_iota(jnp.int32, (tail_rows, HDIM), 0)
+        ends = jnp.zeros((tail_rows, HDIM), jnp.int32)
+        row_asked = lax.broadcasted_iota(jnp.int32, (ask_rows, HDIM), 0)
+        starts = member * asking + lax.rem(row_asked, asking)
+        for s in range(slots):
+            ends = jnp.where(row == s, len_ref[s] + (asking * 2**bits - 1), ends)
+            starts = starts + jnp.where(row_asked // asking == s, len_ref[s], 0)
+        acos_ref[:tail_rows], asin_ref[:tail_rows] = turn(ends)
+        acos_ref[tail_rows:], asin_ref[tail_rows:] = turn(starts)
+
+    for block in range(AHEAD):
+        weight_event(0, block)
     for i in range(-lead, 0):
         for e in range(lead):
-            block = i + lead - e
+            block = i + lead - e + (AHEAD if e == 0 else 0)
             if block >= 0:
                 weight_event(e, block)
         if i == -lead:
+            tables()
             for copy in loads:
                 copy.wait()
+
+            @pl.when(ones(tail_order) == 1)
+            def _():
+                for r in range(tail_rows // strip):
+                    rows = []
+                    for s in range(r * strip, (r + 1) * strip):
+                        rows.append(asked_rows(min(s, slots - 1))[asking - 1 :])
+                    normed[held + r * strip : held + (r + 1) * strip, :] = jnp.concatenate(
+                        rows, axis=0
+                    ).astype(normed.dtype)
 
             @pl.loop(0, ask_rows // strip)
             def _(r):
                 rows = pl.ds(pl.multiple_of(held + tail_rows + r * strip, strip), strip)
-                normed[rows, :] = scaled(normed[rows, :])
+                each = strip // asking
+                normed[rows, :] = scaled(
+                    jnp.concatenate([asked_rows(r * each + k) for k in range(each)], axis=0)
+                )
 
         norm_slots(cuts[i + lead], cuts[i + lead + 1])
         t = i + lead
@@ -302,12 +362,14 @@
         pl.when(tail_gives(t))(lambda: tail_copy(t).start())
     pl.when(tail_gets(bits - 1))(lambda: tail_copy(bits - 1).wait_recv())
 
+    for t in range(bits):
+        pl.when(tail_gives(t))(lambda: tail_copy(t).wait_send())
     for r in range(tail_rows // strip):
-        normed[held + r * strip : held + (r + 1) * strip, :] = scaled(
-            tail_raw[r * strip : (r + 1) * strip, :]
-        )
-
-    repeat = piece_rows // chunk
+        rows = slice(held + r * strip, held + (r + 1) * strip)
+        normed[rows, :] = scaled(normed[rows, :])
+
+    tile_rows = held // tiles
+    repeat = tile_rows // chunk
 
     def piece(block, start, rows, tail):
         x = normed[pl.ds(start, rows), :]
@@ -329,7 +391,7 @@
                 ).astype(result.dtype)
             if tail:
                 result[block, held : held + tail, columns] = turn(
-                    raw[piece_rows:, columns], acos_ref[:tail, :], asin_ref[:tail, :]
+                    raw[tile_rows:, columns], acos_ref[:tail, :], asin_ref[:tail, :]
                 ).astype(result.dtype)
 
     each = piece_rows // chunk
@@ -369,10 +431,10 @@
                 )
 
             seen = jnp.full((chunk, used), NEG, jnp.float32)
-            for p in range(pieces):
-                logits = logits_of(p * piece_rows, (p + 1) * piece_rows)
-                for u in range(each):
-                    s = p * each + u
+            for p in range(tiles):
+                logits = logits_of(p * tile_rows, (p + 1) * tile_rows)
+                for u in range(repeat):
+                    s = p * repeat + u
                     alive = (slot == s) & (token < len_ref[s])
                     seen = jnp.where(alive, logits[u * chunk : (u + 1) * chunk], seen)
             logits = logits_of(held, held + ask_rows)
@@ -424,7 +486,7 @@
     def score_copy(step):
         return pltpu.make_async_remote_copy(
             src_ref=stat.at[bits],
-            dst_ref=stat_hbm.at[corpus],
+            dst_ref=stat_all.at[corpus],
             send_sem=stat_sem.at[0, bits + step],
             recv_sem=stat_sem.at[1, bits + step],
             device_id={"corpus": lax.rem(corpus + step, n_corpus)},
@@ -433,7 +495,7 @@
 
     def score_own():
         return pltpu.make_async_copy(
-            stat.at[bits], stat_hbm.at[corpus], stat_sem.at[0, bits + n_corpus]
+            stat.at[bits], stat_all.at[corpus], stat_sem.at[0, bits + n_corpus]
         )
 
     def merge_stats():
@@ -465,6 +527,8 @@
         corner = (p,) + (0,) * (bits - t) + (slice(None),) * t
         token = member * chunk + lax.broadcasted_iota(jnp.int32, (chunk, width), 0)
         allowed = lax.broadcasted_iota(jnp.int32, (chunk, width), 1) <= token
+        keep = member * chunk + lax.broadcasted_iota(jnp.int32, (chunk, HDIM), 0)
+        keep = keep < len_ref[p * each + u]
         for head in range(KVHEADS):
             spots = [spot(head * GROUP + g) for g in range(GROUP)]
             query = jnp.concatenate(
@@ -487,7 +551,9 @@
             )
             context = context.reshape(GROUP, chunk, HDIM) * inverse
             for g, (block, columns) in enumerate(spots):
-                result[pair_blocks + block, rows, columns] = context[g].astype(result.dtype)
+                result[pair_blocks + block, rows, columns] = jnp.where(
+                    keep, context[g], 0.0
+                ).astype(result.dtype)
 
     def context_copy(p, j):
         rows = pl.ds(pl.multiple_of(p * piece_rows, 16), piece_rows)
@@ -511,38 +577,38 @@
         for j in range(blocks - pair_blocks):
             context_copy(p, j).start()
 
-    begin = max(blocks - pair_steps - 1, pair_blocks)
-    finish = begin + pieces + pair_steps
+    begin = pair_blocks + WAIT
+    finish = max(begin + pair_steps, blocks) + pieces
 
     @pl.loop(0, finish)
     def _(i):
         for e in range(weight_steps + 1):
-            block = i + lead - e
+            block = i + lead - e + (AHEAD if e == 0 else 0)
 
             @pl.when(block < blocks)
             def _():
                 weight_event(e, block)
 
-        for e in range(pair_steps + 1):
-            place_of = i - begin - e
-
-            @pl.when((place_of >= 0) & (place_of < pieces))
-            def _():
-                pair_event(e, place_of)
+            if e <= pair_steps:
+                part = i - begin - e
+
+                @pl.when((part >= 0) & (part < pieces))
+                def _():
+                    pair_event(e, part)
 
         @pl.when(i < blocks)
         def _():
-            @pl.loop(0, pieces - 1)
+            @pl.loop(0, tiles - 1)
             def _(t):
-                piece(i, pl.multiple_of(t * piece_rows, 16), piece_rows, 0)
+                piece(i, pl.multiple_of(t * tile_rows, 16), tile_rows, 0)
 
         @pl.when(i < pair_blocks)
         def _():
-            piece(i, held - piece_rows, piece_rows + tail_rows + ask_rows, tail_rows + ask_rows)
+            piece(i, held - tile_rows, tile_rows + tail_rows + ask_rows, tail_rows + ask_rows)
 
         @pl.when((i >= pair_blocks) & (i < blocks))
         def _():
-            piece(i, held - piece_rows, piece_rows + tail_rows, tail_rows)
+            piece(i, held - tile_rows, tile_rows + tail_rows, tail_rows)
 
         @pl.when(i == pair_blocks - 1)
         def _():
@@ -557,15 +623,30 @@
         def _():
             merge_stats()
 
-        done = i - begin - pair_steps
-
-        @pl.when(done >= 0)
+        late = max(begin + pair_steps, blocks)
+        done = i - late
+
+        @pl.when((done >= 0) & (done < pieces))
         def _():
             attend_piece(done)
 
     for step in range(1, n_corpus):
         score_copy(step).wait()
     score_own().wait()
+    pair_dev = pair_group // 2**bits
+    first = corpus * pair_group
+    for d in range(pair_dev):
+        own = member * pair_dev + d
+        name = owner_ref[first + own]
+
+        def count(q, value):
+            return value + jnp.where((owner_ref[first + q] == name) & (q < own), 1, 0)
+
+        slot = corpus * CAP + lax.fori_loop(0, pair_group, count, jnp.int32(0))
+        sums = stat_all[name]
+        ratio = sums[2 * KVHEADS : 3 * KVHEADS, :used] / sums[KVHEADS : 2 * KVHEADS, :used]
+        lane = lax.rem(lax.broadcasted_iota(jnp.int32, ratio.shape, 1), tail_rows)
+        score_ref[d] = jnp.sum(jnp.where(lane == slot, ratio, 0.0))
     for t in range(bits):
         stat_copy(t).wait_send()
 
@@ -583,25 +664,26 @@
         for j in range(blocks - pair_blocks):
             context_copy(p, j).wait()
 
-    for t in range(bits):
-        pl.when(tail_gives(t))(lambda: tail_copy(t).wait_send())
-
-
-def fused(ids, lengths, store, ask, tail, gain, wk, wv, wq, tables, gains, bits, n_corpus):
-    slots = ids.shape[0]
-    pieces = n_corpus
+
+def fused(owners, picks, asks, block_lengths, store, queries, gain, wk, wv, wq, inverse, gains, bits, n_corpus):
+    slots = n_corpus * CAP
+    asking = queries.shape[1]
+    tail_rows = pl.cdiv(slots, 16) * 16
+    ask_rows = slots * asking
+    pair_dev = owners.shape[0] // n_corpus // 2**bits
+    pieces = slots // 2
     _, chunk, depth = store.shape
     own_rows = wq.shape[0]
     key_blocks = wk.shape[1] // WIDE
     pair_blocks = key_blocks + wv.shape[1] // WIDE
     blocks = pair_blocks + wq.shape[1] // WIDE
     held = slots * chunk
-    total = held + tail.shape[0] + ask.shape[0]
+    total = held + tail_rows + ask_rows
     piece_rows = held // pieces
     stages = bits - 1
     cube = (2,) * bits
-    lanes = pl.cdiv(GROUP * tail.shape[0], 128) * 128
-    plan = (bits, slots, pieces, key_blocks, pair_blocks, blocks, n_corpus)
+    lanes = pl.cdiv(GROUP * tail_rows, 128) * 128
+    plan = (bits, slots, pieces, n_corpus, key_blocks, pair_blocks, blocks, n_corpus)
     whole = pl.BlockSpec(memory_space=pltpu.VMEM)
     apart = pl.BlockSpec(memory_space=pl.ANY)
     scalar = pl.BlockSpec(memory_space=pltpu.SMEM)
@@ -609,20 +691,27 @@
         functools.partial(gather_project_kernel, plan),
         out_shape=(
             jax.ShapeDtypeStruct((held, wq.shape[1]), store.dtype),
-            jax.ShapeDtypeStruct((n_corpus, 8, lanes), jnp.float32),
+            jax.ShapeDtypeStruct((pair_dev,), jnp.float32),
         ),
-        in_specs=[scalar, scalar, apart, apart, apart, whole, apart, apart, apart]
-        + [whole] * (len(tables) + 1),
-        out_specs=(apart, apart),
+        in_specs=[scalar] * 4 + [apart, apart, whole, apart, apart, apart, whole, whole],
+        out_specs=(apart, scalar),
         scratch_shapes=[
+            pltpu.SMEM((slots,), jnp.int32),
+            pltpu.SMEM((slots,), jnp.int32),
+            pltpu.SMEM((slots,), jnp.int32),
             pltpu.VMEM(store.shape, store.dtype),
+            pltpu.VMEM(queries.shape, store.dtype),
             pltpu.VMEM((total, depth), store.dtype),
             pltpu.VMEM((blocks,) + cube + (own_rows, WIDE), store.dtype),
-            pltpu.VMEM(tail.shape, store.dtype),
             pltpu.VMEM((blocks, total, WIDE), store.dtype),
             pltpu.VMEM((pieces,) + cube + (pair_blocks, piece_rows, WIDE), store.dtype),
+            pltpu.VMEM((chunk, HDIM), jnp.float32),
+            pltpu.VMEM((chunk, HDIM), jnp.float32),
+            pltpu.VMEM((tail_rows + ask_rows, HDIM), jnp.float32),
+            pltpu.VMEM((tail_rows + ask_rows, HDIM), jnp.float32),
             pltpu.VMEM((bits + 1, 8, lanes), jnp.float32),
             pltpu.VMEM((bits, 8, lanes), jnp.float32),
+            pltpu.VMEM((n_corpus, 8, lanes), jnp.float32),
             pltpu.SemaphoreType.DMA((5,)),
             pltpu.SemaphoreType.DMA((blocks,)),
             pltpu.SemaphoreType.DMA((pieces,)),
@@ -640,7 +729,7 @@
             transcendentals=0,
             bytes_accessed=2 * (total * depth + depth * blocks * WIDE),
         ),
-    )(ids, lengths, store, ask, tail, gain, wk, wv, wq, *tables, gains)
+    )(owners, picks, asks, block_lengths, store, queries, gain, wk, wv, wq, inverse, gains)
 
 
 def on_device(
@@ -657,95 +746,27 @@
     w_score,
 ):
     n_corpus = lax.axis_size("corpus")
-    n_rerank = lax.axis_size("rerank")
-    corpus_index = lax.axis_index("corpus")
-    member = lax.axis_index("rerank")
-
-    pair_total = cand_block.shape[0]
-    pair_group = pair_total // n_corpus
-    pair_dev = pair_group // n_rerank
-    own_blocks, chunk, depth = store_rows.shape
-    asking = queries.shape[1]
-    owners = cand_owner[:, 0]
-    pair_order = jnp.arange(pair_total, dtype=jnp.int32)
-    group_of = pair_order // pair_group
-    earlier = (
-        (owners[:, None] == owners[None, :])
-        & (group_of[:, None] == group_of[None, :])
-        & (pair_order[None, :] < pair_order[:, None])
-    )
-    owner_rank = jnp.sum(earlier.astype(jnp.int32), axis=1)
-    slots = n_corpus * CAP
-    slot_ids = jnp.arange(slots, dtype=jnp.int32)
-    wanted = (owners == corpus_index)[None, :] & (
-        (group_of * CAP + owner_rank)[None, :] == slot_ids[:, None]
-    )
-
-    def per_slot(values):
-        return jnp.sum(jnp.where(wanted, values[None, :], 0), axis=1)
-
-    block_ids = per_slot(cand_block)
-    query_ids = per_slot(cand_query)
-    own_lengths = lax.dynamic_slice(block_lengths, (corpus_index * own_blocks,), (own_blocks,))
-    chosen = block_ids[:, None] == jnp.arange(own_blocks, dtype=jnp.int32)[None, :]
-    lengths = jnp.sum(jnp.where(chosen, own_lengths[None, :], 0), axis=1)
-    lengths = jnp.where(jnp.any(wanted, axis=1), lengths, 0)
-
-    gain = norm_gain[None, :]
-    held = slots * chunk
-    ask = jnp.take(queries, query_ids, axis=0).reshape(slots * asking, depth)
-    tail = jnp.take(queries.reshape(-1, depth), query_ids * asking + asking - 1, axis=0)
-    tail_rows = pl.cdiv(slots, 16) * 16
-    tail = jnp.pad(tail, ((0, tail_rows - slots), (0, 0)))
-    ends = jnp.pad(lengths + (n_rerank * asking - 1), (0, tail_rows - slots))
-    here = member * chunk + jnp.arange(chunk, dtype=jnp.int32)
-    there = lengths[:, None] + (member * asking + jnp.arange(asking, dtype=jnp.int32))[None, :]
-    positions = jnp.concatenate([here, ends, there.reshape(-1)])
+    bits = lax.axis_size("rerank").bit_length() - 1
     half = HDIM // 2
     inverse = jnp.power(ROPE_BASE, -2.0 * jnp.arange(half, dtype=jnp.float32) / HDIM)
-    angles = positions.astype(jnp.float32)[:, None] * inverse
-    cosine = jnp.cos(angles)
-    sine = jnp.sin(angles)
-    cosine = jnp.concatenate([cosine, cosine], axis=1)
-    sine = jnp.concatenate([-sine, sine], axis=1)
-    tables = (cosine[:chunk], sine[:chunk], cosine[chunk:], sine[chunk:])
-    bits = n_rerank.bit_length() - 1
-    gains = w_score.reshape(QHEADS, HDIM)
-    context, stats = fused(
-        block_ids,
-        lengths,
+    inverse = jnp.concatenate([inverse, inverse])[None, :]
+    context, scores = fused(
+        cand_owner[:, 0],
+        cand_block,
+        cand_query,
+        block_lengths,
         store_rows,
-        ask,
-        tail,
-        gain,
+        queries,
+        norm_gain,
         w_key,
         w_value,
         w_query,
-        tables,
-        gains,
+        inverse,
+        w_score.reshape(QHEADS, HDIM),
         bits,
         n_corpus,
     )
-    wide = context.shape[1]
-    here = member * chunk + jnp.arange(chunk, dtype=jnp.int32)
-    keep = here[None, :, None] < lengths[:, None, None]
-    context = jnp.where(keep, context.reshape(slots, chunk, wide), 0)
-    used = GROUP * tail_rows
-    ratio = stats[:, 2 * KVHEADS : 3 * KVHEADS, :used] / stats[:, KVHEADS : 2 * KVHEADS, :used]
-    ratio = ratio.reshape(n_corpus, KVHEADS * GROUP, tail_rows).sum(axis=1)[:, :slots]
-    first = corpus_index * pair_group + member * pair_dev
-    mine = first + jnp.arange(pair_dev, dtype=jnp.int32)
-    is_mine = mine[:, None] == pair_order[None, :]
-
-    def of_mine(values):
-        return jnp.sum(jnp.where(is_mine, values[None, :], 0), axis=1)
-
-    place = of_mine(owners) * slots + corpus_index * CAP + of_mine(owner_rank)
-    spread = jnp.arange(n_corpus * slots, dtype=jnp.int32)
-    scores = jnp.sum(
-        jnp.where(place[:, None] == spread[None, :], ratio.reshape(1, -1), 0.0), axis=1
-    )
-    return (context, scores)
+    return (context.reshape(n_corpus * CAP, store_rows.shape[1], context.shape[1]), scores)
 
 
 def solution(mesh):

time: 149 us -> 132 us (0.89); the launches traced: 147 us -> 132 us
  other arithmetic: 13.9 us -> 0.6 us
    select_n x5 -> x0, other arithmetic: 6.1 us -> none  [the longest x1 4.84 us: on_device(): context = jnp.where(keep, context.reshape(slots, chunk, wide), 0)]
    unnamed x10 -> x4, local copies, waits for them, and re-layouts: 0.3 us -> 5.42 us
    reduce_sum x6 -> x0, other arithmetic: 3.48 us -> none  [the longest x1 0.92 us: on_device(): owner_rank = jnp.sum(earlier.astype(jnp.int32), axis=1)]
    gather x2 -> x0, local copies, waits for them, and re-layouts: 3.26 us -> none  [the longest x1 2.64 us: on_device(): jnp.take(queries.reshape(-1, depth), query_ids * asking + asking - 1, axi...]
    broadcast_in_dim x4 -> x0, local copies, waits for them, and re-layouts: 1.57 us -> none  [the longest x1 1.31 us: on_device(): gain = norm_gain[None, :]]
where the time goes in v3:
time: 132 us
  Pallas kernels  125 us (95%)
  local copies, waits for them, and re-layouts  5.42 us (4%)
    pallas_call x1, Pallas kernels, fused(): pl.pallas_call(functools.partial(gather_project_kernel, plan), out_shape=...  125 us
    unnamed x4, local copies, waits for them, and re-layouts  5.42 us

profile of v3, /device:TPU:28, one launch (start us, length us, event | category | flops | bytes accessed | tf_op | source)
XLA Modules:
  0.0 131.6 jit_solution(17548245737405590081)
XLA Ops:
  0.6 0.6 maximum_bitcast_fusion.inverse_ref
  1.2 124.9 %shard_map.122 = (bf16[1280,1792]{1,0:T(8,128)(2,1)}, f32[2]{0:T(128)}) custom-call(s32[64]{0:T(128)} %bitcast.7, s32[64]{0:T(128)} %pick_ref.1, s32[64]{0:T(128)} %ask_ref.1, s32[128]{0:T(128)} %length_ref.1, bf16[32,64,3584]{2,1,0:T(8,128)(2,1)} %store_hbm.1, bf16[32,8,3584]{2,1,0:T(8,128)(2,1)} %query_hbm.1, bf16[3584]{0:T(1024)(128)(2,1)} %gain_ref.1, ...), custom_call_target="tpu_custom_call" | custom-call | flops 24310185984 | bytes 27066368 | tf_op jit(solution)/shard_map/pallas_call | solution.py:690
  126.2 0.0 copy-start
  126.2 4.9 %copy.15 = bf16[20,64,1792]{2,1,0:T(8,128)(2,1)} copy(bf16[20,64,1792]{2,1,0:T(8,128)(2,1)} %bitcast.5) | data formatting | bytes 9175040
  131.1 0.0 copy-done
  131.1 0.5 copy.16
  (1 shorter events, 0.0 us)
Async XLA Ops:
  126.2 4.9 %copy-start = (f32[2]{0:T(128)S(1)}, f32[2]{0:T(128)}, u32[]{:S(2)}) copy-start(f32[2]{0:T(128)} %get-tuple-element.9) | copy-start | bytes 28

commit v4 on v3

--- a/solution.py
+++ b/solution.py
@@ -732,6 +732,42 @@
     )(owners, picks, asks, block_lengths, store, queries, gain, wk, wv, wq, inverse, gains)
 
 
+def hand_over_kernel(parts, source, target, held, in_sem, out_sem):
+    rows = source.shape[0] // parts
+
+    def copies(c):
+        span = pl.ds(c * rows, rows)
+        return (
+            pltpu.make_async_copy(source.at[span], held.at[span], in_sem.at[c]),
+            pltpu.make_async_copy(held.at[span], target.at[span], out_sem.at[c]),
+        )
+
+    for c in range(parts):
+        copies(c)[0].start()
+    for c in range(parts):
+        taken, put = copies(c)
+        taken.wait()
+        put.start()
+    for c in range(parts):
+        copies(c)[1].wait()
+
+
+def hand_over(values, parts):
+    apart = pl.BlockSpec(memory_space=pl.ANY)
+    return pl.pallas_call(
+        functools.partial(hand_over_kernel, parts),
+        out_shape=jax.ShapeDtypeStruct(values.shape, values.dtype),
+        in_specs=[apart],
+        out_specs=apart,
+        scratch_shapes=[
+            pltpu.VMEM(values.shape, values.dtype),
+            pltpu.SemaphoreType.DMA((parts,)),
+            pltpu.SemaphoreType.DMA((parts,)),
+        ],
+        compiler_params=pltpu.CompilerParams(vmem_limit_bytes=VMEM),
+    )(values)
+
+
 def on_device(
     store_rows,
     block_lengths,
@@ -766,6 +802,7 @@
         bits,
         n_corpus,
     )
+    context = hand_over(context, n_corpus * CAP // 2)
     return (context.reshape(n_corpus * CAP, store_rows.shape[1], context.shape[1]), scores)
 
 

time: 132 us -> 132 us (level)
  local copies, waits for them, and re-layouts: 5.42 us -> 1.17 us
  Pallas kernels: 125 us -> 129 us
    unnamed x4 -> x1, local copies, waits for them, and re-layouts: 5.42 us -> 1.17 us
    pallas_call x0 -> x1, Pallas kernels: none -> 4.06 us  [hand_over(): pl.pallas_call(functools.partial(hand_over_kernel, parts), out_shape=jax....]
where the time goes in v4:
time: 132 us; the launch traced here: 131 us
  Pallas kernels  129 us (98%)
    pallas_call x1, Pallas kernels, fused(): pl.pallas_call(functools.partial(gather_project_kernel, plan), out_shape=...  125 us
    pallas_call x1, Pallas kernels, hand_over(): pl.pallas_call(functools.partial(hand_over_kernel, parts), out_shape=jax....  4.06 us

profile of v4, /device:TPU:28, one launch (start us, length us, event | category | flops | bytes accessed | tf_op | source)
XLA Modules:
  0.0 131.4 jit_solution(3623595590426062431)
XLA Ops:
  0.6 0.6 maximum_bitcast_fusion.inverse_ref
  1.2 124.9 %shard_map.122 = (bf16[1280,1792]{1,0:T(8,128)(2,1)}, f32[2]{0:T(128)}) custom-call(s32[64]{0:T(128)} %bitcast.7, s32[64]{0:T(128)} %pick_ref.1, s32[64]{0:T(128)} %ask_ref.1, s32[128]{0:T(128)} %length_ref.1, bf16[32,64,3584]{2,1,0:T(8,128)(2,1)} %store_hbm.1, bf16[32,8,3584]{2,1,0:T(8,128)(2,1)} %query_hbm.1, bf16[3584]{0:T(1024)(128)(2,1)} %gain_ref.1, ...), custom_call_target="tpu_custom_call" | custom-call | flops 24310185984 | bytes 27066368 | tf_op jit(solution)/shard_map/pallas_call | solution.py:690
  126.1 4.1 %shard_map.123 = bf16[1280,1792]{1,0:T(8,128)(2,1)} custom-call(bf16[1280,1792]{1,0:T(8,128)(2,1)} %get-tuple-element.4.source), custom_call_target="tpu_custom_call" | custom-call | tf_op jit(solution)/shard_map/pallas_call | solution.py:757
  130.2 1.2 copy.14
  (1 shorter events, 0.0 us)
